TPU v7x, 32 devices: a whole 2x2x4 slice. The times are simulated.
32 devices in a mesh: dp: 4 (over x, core), seq: 8 (over z, y).
Axes of the slice: x: 2, y: 2, z: 4, core: 2. Of those that a mesh axis runs over, the one named last changes fastest.
Arguments:
- q_raw: bfloat16 [4, 1024, 4096], P('dp', 'seq'), may hold values from -64 to 64
- k_raw: bfloat16 [4, 1024, 4096], P('dp', 'seq'), may hold values from -64 to 64
- values: bfloat16 [4, 1024, 4096], P('dp', 'seq'), may hold values from -6 to 6
- grad_out: bfloat16 [4, 1024, 4096], P('dp', 'seq'), may hold values from -6 to 6
- q_gain: float32 [4096], replicated, may hold values from 0.1 to 1.9
- k_gain: float32 [4096], replicated, may hold values from 0.1 to 1.9
- lengths: int32 [4, 6], P('dp'), may hold values from 1 to 341, 1024 in all within a row
- positions: int32 [4, 3, 1024], P('dp', None, 'seq'), may hold values from 0 to 63
Outputs:
- attended: bfloat16 [4, 1024, 4096], P('dp', 'seq')
- grad_q: bfloat16 [4, 1024, 4096], P('dp', 'seq')
- grad_k: bfloat16 [4, 1024, 4096], P('dp', 'seq')
- grad_v: bfloat16 [4, 1024, 4096], P('dp', 'seq')
- grad_q_gain: float32 [4096], replicated
- grad_k_gain: float32 [4096], replicated
Inputs may be any that keep to these rules, and one draw needn't show every extreme that they name: `lengths`: the clips of a bucket lie end to end and fill its 1024 tokens.
All inputs are finite; a program needn't handle non-finite values.
Results may differ from a plain program's by a relative error of at most 0.012.
The roundings to bfloat16 on the way count: a program that leaves them out, or rounds other values in their place, can miss the bound.
Values may be sent and summed in bfloat16 or wider, within the bound.
A program may use at most 128 MiB of HBM per device.

v0:
```python
import functools

import jax
import jax.numpy as jnp
import numpy as np
from jax import lax
from jax.experimental import pallas as pl
from jax.experimental.pallas import tpu as pltpu
from jax.sharding import PartitionSpec as P

HEAD_DIM = 128
LANES = 128
QUERY_BLOCK = 256
GROUPS = 4
ATTEND_LAG = 2
DISTRIBUTE_LAG = 2
EPSILON = 1e-06
MESH = pl.DeviceIdType.MESH


def rope_tables(position_rows, head_dim):
    half = head_dim // 2
    sixth = head_dim // 6
    first = half - 2 * sixth
    pairs = np.arange(head_dim) % half
    section = (pairs >= first).astype(np.int32) + (pairs >= first + sixth).astype(np.int32)
    begin = np.where(section == 0, 0, np.where(section == 1, first, first + sixth))
    number = np.where(section == 0, first, sixth)
    freqs = (10000.0 ** (-(pairs - begin) / number)).astype(np.float32)
    sign = np.where(np.arange(head_dim) < half, -1.0, 1.0).astype(np.float32)
    rows = position_rows.astype(jnp.float32)[:, :, None]
    chosen = jnp.where(section == 0, rows[0], jnp.where(section == 1, rows[1], rows[2]))
    angle = chosen * freqs
    return jnp.cos(angle), jnp.sin(angle) * sign


def dot(left, right, left_dim, right_dim):
    return lax.dot_general(
        left, right, (((left_dim,), (right_dim,)), ((), ())), preferred_element_type=jnp.float32
    )


def kernel(
    sizes,
    len_ref, q_ref, k_ref, v_ref, do_ref, gq_ref, gk_ref, cos_ref, sin_ref,
    out_ref, gain_ref,
    beside, sent, recv, back, key_acc, value_acc, scale_q, scale_k,
    part, seq_part, dp_sum, dp_part, total,
    in_send, in_recv, own_sem, out_send, out_recv, gain_send, gain_recv,
    halo_send, halo_recv, beside_send, beside_recv,
):
    n, replicas, heads, tok, clips, reach, halo, padded = sizes
    members = n // GROUPS
    group_tokens = members * tok
    group_end = halo + group_tokens
    window = group_end + halo
    feature = members * heads * HEAD_DIM
    ratio = GROUPS
    shared = heads // ratio
    me = lax.axis_index("seq")
    side = me // members
    place_in = lax.rem(me, members)
    my_dp = lax.axis_index("dp")
    scale = HEAD_DIM ** (-0.5)

    def peer(step):
        return lax.rem(me + step, n)

    def member(step):
        return lax.rem(place_in + step, members)

    def device(group, index):
        return (my_dp, group * members + index)

    def columns(owner, head):
        return pl.ds(pl.multiple_of((owner * heads + head) * HEAD_DIM, HEAD_DIM), HEAD_DIM)

    def rows(owner):
        return pl.ds(pl.multiple_of(halo + owner * tok, 16), tok)

    def each_side(act):
        @pl.when(side > 0)
        def _():
            act(0, side - 1)

        @pl.when(side < GROUPS - 1)
        def _():
            act(1, side + 1)

    def remote(src, dst, send_sem, recv_sem, device):
        return pltpu.make_async_remote_copy(
            src_ref=src, dst_ref=dst, send_sem=send_sem, recv_sem=recv_sem,
            device_id=device, device_id_type=MESH,
        )

    barrier = pltpu.get_barrier_semaphore()
    for step in range(1, n):
        pl.semaphore_signal(barrier, inc=1, device_id=(my_dp, peer(step)), device_id_type=MESH)
    for step in range(1, replicas):
        other = lax.rem(my_dp + step, replicas)
        pl.semaphore_signal(barrier, inc=1, device_id=(other, me), device_id_type=MESH)
    pl.semaphore_wait(barrier, n - 1 + replicas - 1)

    def send_values(head):
        cols = columns(place_in, head)
        for place, ref in ((2, v_ref), (3, do_ref)):
            pltpu.make_async_copy(
                ref.at[:, cols], recv.at[head, place, rows(place_in), :], own_sem.at[head]
            ).start()

        @pl.loop(1, members)
        def _(step):
            other = member(step)
            for place, ref in ((2, v_ref), (3, do_ref)):
                remote(
                    ref.at[:, columns(other, head)], recv.at[head, place, rows(place_in), :],
                    in_send.at[head], in_recv.at[head], device(side, other),
                ).start()

    send_values(0)

    def squares(index, sums):
        cols = pl.ds(pl.multiple_of(index * LANES, LANES), LANES)
        query = q_ref[:, cols].astype(jnp.float32)
        keys = k_ref[:, cols].astype(jnp.float32)
        return sums[0] + query * query, sums[1] + keys * keys

    zero = jnp.zeros((tok, LANES), jnp.float32)
    sum_q, sum_k = lax.fori_loop(0, feature // LANES, squares, (zero, zero))
    for sums, target in ((sum_q, scale_q), (sum_k, scale_k)):
        mean = jnp.sum(sums, axis=1, keepdims=True) / feature
        target[...] = jnp.broadcast_to(lax.rsqrt(mean + EPSILON), (tok, LANES))

    def rotated(ref, gain, norm, cols):
        x = ref[:, cols].astype(jnp.float32) * norm[...] * gain[:, cols]
        turned = x * cos_ref[...] + pltpu.roll(x, HEAD_DIM // 2, 1) * sin_ref[...]
        return turned.astype(jnp.bfloat16)

    @pl.loop(0, heads)
    def _(head):
        @pl.when(head > 0)
        def _():
            send_values(head)

        @pl.loop(1, members)
        def _(step):
            other = member(step)
            cols = columns(other, head)
            sent[head, other, 0] = rotated(q_ref, gq_ref, scale_q, cols)
            sent[head, other, 1] = rotated(k_ref, gk_ref, scale_k, cols)
            remote(
                sent.at[head, other], recv.at[head, 0:2, rows(place_in), :],
                in_send.at[head], in_recv.at[head], device(side, other),
            ).start()

        cols = columns(place_in, head)
        for place, (ref, gain, norm) in enumerate(((q_ref, gq_ref, scale_q), (k_ref, gk_ref, scale_k))):
            recv[head, place, rows(place_in), :] = rotated(ref, gain, norm, cols)

    bounds = []
    running = len_ref[0, 0]
    for clip in range(clips):
        bounds.append(running)
        if clip + 1 < clips:
            running = running + len_ref[0, clip + 1]

    def edges(middle):
        first, last = jnp.int32(0), jnp.int32(n * tok)
        for bound in bounds:
            first = jnp.maximum(first, jnp.where(bound <= middle, bound, 0))
            last = jnp.minimum(last, jnp.where(bound > middle, bound, n * tok))
        low_owns = last - middle <= middle - first
        return jnp.where(low_owns, middle, first), jnp.where(low_owns, last, middle)

    token_start = side * group_tokens
    high_edge = edges(token_start)[1]
    low_edge = edges(token_start + group_tokens)[0]

    def clear(begin, end):
        @pl.loop(0, heads)
        def _(head):
            recv[head, :, begin:end, :] = jnp.zeros((4, end - begin, HEAD_DIM), jnp.bfloat16)

    if padded > window:
        clear(window, padded)

    @pl.when(side == 0)
    def _():
        clear(0, halo)

    @pl.when(side == GROUPS - 1)
    def _():
        clear(group_end, window)

    def segment(shape, dim, start):
        inside = lax.broadcasted_iota(jnp.int32, shape, dim) + start
        places = inside + (token_start - halo)
        found = jnp.zeros(shape, jnp.int32)
        for bound in bounds:
            found = found + (places >= bound).astype(jnp.int32)
        valid = (inside < window) & (places >= 0) & (places < n * tok)
        return jnp.where(valid, found, -1)

    group_rows = ((halo, halo + halo), (group_end - halo, group_end))
    halo_rows = ((0, halo), (group_end, window))

    def relay(head):
        arrived = recv.at[head, :, pl.ds(0, (members - 1) * tok), :]
        pltpu.make_async_copy(arrived, arrived, in_recv.at[head]).wait()
        own = recv.at[head, pl.ds(2, 2), pl.ds(0, tok), :]
        pltpu.make_async_copy(own, own, own_sem.at[head]).wait()

        def act(which, group):
            source, target = group_rows[which], halo_rows[1 - which]
            remote(
                recv.at[head, :, source[0]:source[1], :], recv.at[head, :, target[0]:target[1], :],
                halo_send.at[which, head], halo_recv.at[1 - which, head], device(group, place_in),
            ).start()

        each_side(act)

    def attend(head):
        def arrive(which, group):
            target = halo_rows[which]
            held = recv.at[head, :, target[0]:target[1], :]
            pltpu.make_async_copy(held, held, halo_recv.at[which, head]).wait()

        each_side(arrive)
        key_acc[...] = jnp.zeros_like(key_acc)
        value_acc[...] = jnp.zeros_like(value_acc)
        for start in range(0, window, QUERY_BLOCK):
            block = min(QUERY_BLOCK, window - start)
            low = max(0, start - reach) // LANES * LANES
            high = min(padded, -(-(start + block + reach) // LANES) * LANES)
            query = recv[head, 0, start:start + block, :]
            keys = recv[head, 1, low:high, :]
            value_rows = recv[head, 2, low:high, :]
            cot = recv[head, 3, start:start + block, :]
            live = segment((block, 1), 0, start) == segment((1, high - low), 1, low)
            scores = jnp.where(live, dot(query, keys, 1, 1), -1e30)
            highest = jnp.max(scores, axis=1, keepdims=True)
            expon = jnp.exp((scores - highest) * scale)
            probs = expon * (1.0 / jnp.sum(expon, axis=1, keepdims=True))
            half = probs.astype(jnp.bfloat16)
            context = dot(half, value_rows, 1, 0).astype(jnp.bfloat16)
            delta = jnp.sum(
                cot.astype(jnp.float32) * context.astype(jnp.float32), axis=1, keepdims=True
            )
            dprob = dot(cot, value_rows, 1, 1)
            dscore = (probs * (dprob - delta) * scale).astype(jnp.bfloat16)
            back[head, 0, start:start + block, :] = context
            back[head, 1, start:start + block, :] = dot(dscore, keys, 1, 0).astype(jnp.bfloat16)
            key_acc[low:high, :] += dot(dscore, query, 0, 0)
            value_acc[low:high, :] += dot(half, cot, 0, 0)
        back[head, 2] = key_acc[0:window, :].astype(jnp.bfloat16)
        back[head, 3] = value_acc[0:window, :].astype(jnp.bfloat16)

        def act(which, group):
            source = halo_rows[which]
            remote(
                back.at[head, :, source[0]:source[1], :], beside.at[head, 1 - which],
                beside_send.at[which, head], beside_recv.at[1 - which, head],
                device(group, place_in),
            ).start()

        each_side(act)

    def distribute(head):
        def merge(which, group):
            held = beside.at[head, which]
            pltpu.make_async_copy(held, held, beside_recv.at[which, head]).wait()
            begin, end = group_rows[which]
            places = lax.broadcasted_iota(jnp.int32, (halo, HEAD_DIM), 0) + (
                token_start + begin - halo
            )
            outside = (places >= low_edge) if which else (places < high_edge)
            for place in range(4):
                back[head, place, begin:end, :] = jnp.where(
                    outside, beside[head, which, place], back[head, place, begin:end, :]
                )

        each_side(merge)
        cols = columns(place_in, head)

        @pl.loop(1, members)
        def _(step):
            other = member(step)
            remote(
                back.at[head, :, rows(other), :], out_ref.at[:, :, cols],
                out_send.at[head], out_recv.at[head], device(side, other),
            ).start()

        out_ref[:, :, cols] = back[head, :, rows(place_in), :]

    @pl.loop(0, heads + ATTEND_LAG + DISTRIBUTE_LAG)
    def _(step):
        @pl.when(step < heads)
        def _():
            relay(step)

        @pl.when((step >= ATTEND_LAG) & (step < heads + ATTEND_LAG))
        def _():
            attend(step - ATTEND_LAG)

        @pl.when(step >= ATTEND_LAG + DISTRIBUTE_LAG)
        def _():
            distribute(step - ATTEND_LAG - DISTRIBUTE_LAG)

    def turned_back(place, ref, norm, cols):
        grads = out_ref[place, :, cols].astype(jnp.float32)
        turned = grads * cos_ref[...] - pltpu.roll(grads, HEAD_DIM // 2, 1) * sin_ref[...]
        return turned, ref[:, cols].astype(jnp.float32) * norm[...]

    inner = (zero, zero)
    for head in range(heads):
        arrived = out_ref.at[:, :, pl.ds(0, (members - 1) * HEAD_DIM)]
        pltpu.make_async_copy(arrived, arrived, out_recv.at[head]).wait()

        def first_pass(owner, sums):
            cols = columns(owner, head)
            results = []
            for place, (ref, gain, norm) in enumerate(
                ((q_ref, gq_ref, scale_q), (k_ref, gk_ref, scale_k))
            ):
                turned, hat = turned_back(place + 1, ref, norm, cols)
                both = turned * hat
                row = place * shared + head % shared
                part[owner * ratio + head // shared, row:row + 1, :] = jnp.sum(both, axis=0, keepdims=True)
                results.append(sums[place] + both * gain[:, cols])
            return tuple(results)

        inner = lax.fori_loop(0, members, first_pass, inner)

    @pl.loop(1, n)
    def _(step):
        other = peer(step)
        remote(
            part.at[other], seq_part.at[me], gain_send.at[0], gain_recv.at[0], (my_dp, other)
        ).start()

    seq_part[me] = part[me]
    inner_q, inner_k = (
        jnp.broadcast_to(jnp.sum(sums, axis=1, keepdims=True) / feature, (tok, LANES))
        for sums in inner
    )

    def second_pass(index):
        cols = pl.ds(pl.multiple_of(index * LANES, LANES), LANES)
        for place, (ref, gain, norm, mean) in enumerate(
            ((q_ref, gq_ref, scale_q, inner_q), (k_ref, gk_ref, scale_k, inner_k))
        ):
            turned, hat = turned_back(place + 1, ref, norm, cols)
            result = norm[...] * (turned * gain[:, cols] - hat * mean)
            out_ref[place + 1, :, cols] = result.astype(jnp.bfloat16)

    pl.loop(0, feature // LANES)(second_pass)

    def wait_all(ref, count, sem):
        held = ref.at[pl.ds(0, count)]
        pltpu.make_async_copy(held, held, sem).wait()

    wait_all(seq_part, n - 1, gain_recv.at[0])
    dp_sum[...] = jnp.sum(seq_part[...], axis=0)
    for step in range(1, replicas):
        other = lax.rem(my_dp + step, replicas)
        remote(
            dp_sum, dp_part.at[my_dp], gain_send.at[1], gain_recv.at[1], (other, me)
        ).start()
    dp_part[my_dp] = dp_sum[...]
    wait_all(dp_part, replicas - 1, gain_recv.at[1])
    total[...] = jnp.sum(dp_part[...], axis=0) / replicas

    @pl.loop(1, n)
    def _(step):
        other = peer(step)
        remote(
            total, gain_ref.at[me], gain_send.at[2], gain_recv.at[2], (my_dp, other)
        ).start()

    gain_ref[me] = total[...]
    wait_all(gain_ref, n - 1, gain_recv.at[2])

    wait_all(seq_part, n - 1, gain_send.at[0])
    wait_all(dp_part, replicas - 1, gain_send.at[1])
    wait_all(seq_part, n - 1, gain_send.at[2])
    for head in range(heads):
        moved = recv.at[head, :, pl.ds(0, (members - 1) * tok), :]
        pltpu.make_async_copy(moved, moved, in_send.at[head]).wait()
        pltpu.make_async_copy(moved, moved, out_send.at[head]).wait()

        def drain(which, group):
            held = beside.at[head, which]
            pltpu.make_async_copy(held, held, halo_send.at[which, head]).wait()
            pltpu.make_async_copy(held, held, beside_send.at[which, head]).wait()

        each_side(drain)


def on_device(q_raw, k_raw, values, grad_out, q_gain, k_gain, lengths, positions):
    n = lax.axis_size("seq")
    replicas = lax.axis_size("dp")
    tok, feature = q_raw.shape[1:]
    shared = feature // n // HEAD_DIM
    heads = GROUPS * shared
    tokens = n * tok
    reach = tokens // 3 - 1
    halo = -(-((reach + 1) // 2) // 16) * 16
    window = tokens // GROUPS + 2 * halo
    padded = -(-window // LANES) * LANES
    cosine, sine = rope_tables(positions[0], HEAD_DIM)
    sizes = (n, replicas, heads, tok, lengths.shape[1], reach, halo, padded)
    vmem = pl.BlockSpec(memory_space=pltpu.VMEM)
    hbm = pl.BlockSpec(memory_space=pl.ANY)
    gain_rows = (2 * shared, LANES)
    half, full = jnp.bfloat16, jnp.float32
    outs, gains = pl.pallas_call(
        functools.partial(kernel, sizes),
        out_shape=(
            jax.ShapeDtypeStruct((4, tok, feature), half),
            jax.ShapeDtypeStruct((n,) + gain_rows, full),
        ),
        in_specs=[
            pl.BlockSpec(memory_space=pltpu.SMEM), vmem, vmem, hbm, hbm, vmem, vmem, vmem, vmem,
        ],
        out_specs=(vmem, vmem),
        scratch_shapes=[
            pltpu.VMEM((heads, 2, 4, halo, HEAD_DIM), half),
            pltpu.VMEM((heads, n // GROUPS, 2, tok, HEAD_DIM), half),
            pltpu.VMEM((heads, 4, padded, HEAD_DIM), half),
            pltpu.VMEM((heads, 4, window, HEAD_DIM), half),
            pltpu.VMEM((padded, HEAD_DIM), full),
            pltpu.VMEM((padded, HEAD_DIM), full),
            pltpu.VMEM((tok, LANES), full),
            pltpu.VMEM((tok, LANES), full),
            pltpu.VMEM((n,) + gain_rows, full),
            pltpu.VMEM((n,) + gain_rows, full),
            pltpu.VMEM(gain_rows, full),
            pltpu.VMEM((replicas,) + gain_rows, full),
            pltpu.VMEM(gain_rows, full),
            pltpu.SemaphoreType.DMA((heads,)),
            pltpu.SemaphoreType.DMA((heads,)),
            pltpu.SemaphoreType.DMA((heads,)),
            pltpu.SemaphoreType.DMA((heads,)),
            pltpu.SemaphoreType.DMA((heads,)),
            pltpu.SemaphoreType.DMA((3,)),
            pltpu.SemaphoreType.DMA((3,)),
            pltpu.SemaphoreType.DMA((2, heads)),
            pltpu.SemaphoreType.DMA((2, heads)),
            pltpu.SemaphoreType.DMA((2, heads)),
            pltpu.SemaphoreType.DMA((2, heads)),
        ],
        compiler_params=pltpu.CompilerParams(
            collective_id=0, has_side_effects=True, vmem_limit_bytes=56 * 1024 * 1024
        ),
    )(
        lengths, q_raw[0], k_raw[0], values[0], grad_out[0],
        q_gain[None], k_gain[None], cosine, sine,
    )
    gains = gains.reshape(n, 2, shared * HEAD_DIM)
    return (
        outs[0][None], outs[1][None], outs[2][None], outs[3][None],
        gains[:, 0].reshape(feature), gains[:, 1].reshape(feature),
    )


def solution(mesh):
    tokens = P("dp", "seq", None)
    return jax.shard_map(
        on_device,
        mesh=mesh,
        in_specs=(tokens, tokens, tokens, tokens, P(), P(), P("dp", None), P("dp", None, "seq")),
        out_specs=(tokens, tokens, tokens, tokens, P(), P()),
        check_vma=False,
    )
```

profile of v0, /device:TPU:0, one launch (start us, length us, event | category | flops | bytes accessed | tf_op | source)
XLA Modules:
  0.0 165.2 jit_solution(5898242274357154930)
XLA Ops:
  0.6 0.7 convert_element_type.4
  1.3 1.7 %sine_multiply_fusion = (f32[128,128]{1,0:T(8,128)}, f32[128,128]{1,0:T(8,128)}) fusion(f32[128]{0:T(128)} %constant.11.clone, f32[128]{0:T(128)} %constant.10.clone, f32[128]{0:T(128)S(1)} %get-tuple-element.19, f32[128]{0:T(128)S(1)} %get-tuple-element.20, f32[128]{0:T(128)S(1)} %get-tuple-element.18, pred[128]{0:T(512)(128)(4,1)} %constant.8.clone, ...), kind=kLoop, calls=%fused_computation | loop fusion | flops 65536 | bytes 133888 | tf_op jit(solution)/shard_map/mul | solution.py:34
  3.0 157.2 %shard_map.163 = (bf16[4,128,4096]{2,1,0:T(8,128)(2,1)}, f32[8,8,128]{2,1,0:T(8,128)}) custom-call(s32[1,6]{1,0:T(1,128)} %len_ref.1, bf16[128,4096]{1,0:T(8,128)(2,1)} %bitcast.14, bf16[128,4096]{1,0:T(8,128)(2,1)} %bitcast.15, bf16[128,4096]{1,0:T(8,128)(2,1)} %bitcast.16, bf16[128,4096]{1,0:T(8,128)(2,1)} %bitcast.17, f32[1,4096]{1,0:T(1,128)} %bitcast.18, ...), custom_call_target="tpu_custom_call" | custom-call | tf_op jit(solution)/shard_map/pallas_call | solution.py:416
  160.3 0.0 copy-start
  160.3 4.3 %fusion.1 = (bf16[1,128,4096]{2,1,0:T(8,128)(2,1)}, bf16[1,128,4096]{2,1,0:T(8,128)(2,1)}, bf16[1,128,4096]{2,1,0:T(8,128)(2,1)}, bf16[1,128,4096]{2,1,0:T(8,128)(2,1)}) fusion(bf16[4,128,4096]{2,1,0:T(8,128)(2,1)} %get-tuple-element.8), kind=kLoop, calls=%fused_computation.6 | loop fusion | bytes 8388608 | tf_op jit(solution)/shard_map/slice | solution.py:461
  164.6 0.0 copy-done
  164.6 0.6 fusion.2
  (2 shorter events, 0.0 us)
Async XLA Ops:
  160.3 4.3 %copy-start = (f32[8,8,128]{2,1,0:T(8,128)S(1)}, f32[8,8,128]{2,1,0:T(8,128)}, u32[]{:S(2)}) copy-start(f32[8,8,128]{2,1,0:T(8,128)} %get-tuple-element.9) | copy-start | bytes 98308
where the time goes:
time: 165 us
  Pallas kernels  157 us (95%)
  local copies, waits for them, and re-layouts  4.95 us (3%)
  other arithmetic  2.39 us (1%)
    pallas_call x1, Pallas kernels, on_device(): pl.pallas_call(functools.partial(kernel, sizes), out_shape=(jax.ShapeDtyp...  157 us
    slice x1, local copies, waits for them, and re-layouts, on_device(): outs[3][None]  4.28 us

commit v1 on v0

--- a/solution.py
+++ b/solution.py
@@ -12,8 +12,10 @@
 LANES = 128
 QUERY_BLOCK = 256
 GROUPS = 4
+CHUNK = 2
+TILE = 16
 ATTEND_LAG = 2
-DISTRIBUTE_LAG = 2
+DISTRIBUTE_LAG = 1
 EPSILON = 1e-06
 MESH = pl.DeviceIdType.MESH
 
@@ -34,6 +36,23 @@
     return jnp.cos(angle), jnp.sin(angle) * sign
 
 
+def slot_sizes(longest, group_tokens, chunk):
+    capacity = TILE
+    while True:
+        sizes = {n: min(group_tokens, capacity // n // TILE * TILE) for n in range(1, chunk + 1)}
+
+        def fits(below, above):
+            return any(
+                (n == 0 or below <= sizes[n]) and (n == chunk or above <= sizes[chunk - n])
+                for n in range(chunk + 1)
+            )
+
+        spill = longest - group_tokens - 1
+        if spill <= sizes[chunk] and all(fits(a, longest - a) for a in range(1, longest)):
+            return capacity, sizes
+        capacity += TILE
+
+
 def dot(left, right, left_dim, right_dim):
     return lax.dot_general(
         left, right, (((left_dim,), (right_dim,)), ((), ())), preferred_element_type=jnp.float32
@@ -44,16 +63,17 @@
     sizes,
     len_ref, q_ref, k_ref, v_ref, do_ref, gq_ref, gk_ref, cos_ref, sin_ref,
     out_ref, gain_ref,
-    beside, sent, recv, back, key_acc, value_acc, scale_q, scale_k,
+    give, take, give_back, take_back, sent, recv, back, key_acc, value_acc, scale_q, scale_k,
     part, seq_part, dp_sum, dp_part, total,
     in_send, in_recv, own_sem, out_send, out_recv, gain_send, gain_recv,
     halo_send, halo_recv, beside_send, beside_recv,
 ):
-    n, replicas, heads, tok, clips, reach, halo, padded = sizes
+    n, replicas, heads, tok, clips, reach, capacity, slots, window, padded = sizes
     members = n // GROUPS
     group_tokens = members * tok
-    group_end = halo + group_tokens
-    window = group_end + halo
+    chunks = heads // CHUNK
+    low = [slots[index + 1] for index in range(CHUNK)]
+    own_end = [below + group_tokens for below in low]
     feature = members * heads * HEAD_DIM
     ratio = GROUPS
     shared = heads // ratio
@@ -75,8 +95,8 @@
     def columns(owner, head):
         return pl.ds(pl.multiple_of((owner * heads + head) * HEAD_DIM, HEAD_DIM), HEAD_DIM)
 
-    def rows(owner):
-        return pl.ds(pl.multiple_of(halo + owner * tok, 16), tok)
+    def rows(owner, index):
+        return pl.ds(pl.multiple_of(low[index] + owner * tok, TILE), tok)
 
     def each_side(act):
         @pl.when(side > 0)
@@ -101,11 +121,11 @@
         pl.semaphore_signal(barrier, inc=1, device_id=(other, me), device_id_type=MESH)
     pl.semaphore_wait(barrier, n - 1 + replicas - 1)
 
-    def send_values(head):
+    def send_values(head, index):
         cols = columns(place_in, head)
         for place, ref in ((2, v_ref), (3, do_ref)):
             pltpu.make_async_copy(
-                ref.at[:, cols], recv.at[head, place, rows(place_in), :], own_sem.at[head]
+                ref.at[:, cols], recv.at[head, place, rows(place_in, index), :], own_sem.at[head]
             ).start()
 
         @pl.loop(1, members)
@@ -113,11 +133,12 @@
             other = member(step)
             for place, ref in ((2, v_ref), (3, do_ref)):
                 remote(
-                    ref.at[:, columns(other, head)], recv.at[head, place, rows(place_in), :],
+                    ref.at[:, columns(other, head)], recv.at[head, place, rows(place_in, index), :],
                     in_send.at[head], in_recv.at[head], device(side, other),
                 ).start()
 
-    send_values(0)
+    for index in range(CHUNK):
+        send_values(index, index)
 
     def squares(index, sums):
         cols = pl.ds(pl.multiple_of(index * LANES, LANES), LANES)
@@ -136,26 +157,32 @@
         turned = x * cos_ref[...] + pltpu.roll(x, HEAD_DIM // 2, 1) * sin_ref[...]
         return turned.astype(jnp.bfloat16)
 
-    @pl.loop(0, heads)
-    def _(head):
-        @pl.when(head > 0)
-        def _():
-            send_values(head)
-
-        @pl.loop(1, members)
-        def _(step):
-            other = member(step)
-            cols = columns(other, head)
-            sent[head, other, 0] = rotated(q_ref, gq_ref, scale_q, cols)
-            sent[head, other, 1] = rotated(k_ref, gk_ref, scale_k, cols)
-            remote(
-                sent.at[head, other], recv.at[head, 0:2, rows(place_in), :],
-                in_send.at[head], in_recv.at[head], device(side, other),
-            ).start()
-
-        cols = columns(place_in, head)
-        for place, (ref, gain, norm) in enumerate(((q_ref, gq_ref, scale_q), (k_ref, gk_ref, scale_k))):
-            recv[head, place, rows(place_in), :] = rotated(ref, gain, norm, cols)
+    @pl.loop(0, chunks)
+    def _(chunk):
+        @pl.when(chunk > 0)
+        def _():
+            for index in range(CHUNK):
+                send_values(chunk * CHUNK + index, index)
+
+        for index in range(CHUNK):
+            head = chunk * CHUNK + index
+
+            @pl.loop(1, members)
+            def _(step):
+                other = member(step)
+                cols = columns(other, head)
+                sent[head, other, 0] = rotated(q_ref, gq_ref, scale_q, cols)
+                sent[head, other, 1] = rotated(k_ref, gk_ref, scale_k, cols)
+                remote(
+                    sent.at[head, other], recv.at[head, 0:2, rows(place_in, index), :],
+                    in_send.at[head], in_recv.at[head], device(side, other),
+                ).start()
+
+            cols = columns(place_in, head)
+            for place, (ref, gain, norm) in enumerate(
+                ((q_ref, gq_ref, scale_q), (k_ref, gk_ref, scale_k))
+            ):
+                recv[head, place, rows(place_in, index), :] = rotated(ref, gain, norm, cols)
 
     bounds = []
     running = len_ref[0, 0]
@@ -164,79 +191,177 @@
         if clip + 1 < clips:
             running = running + len_ref[0, clip + 1]
 
-    def edges(middle):
+    def straddle(middle):
         first, last = jnp.int32(0), jnp.int32(n * tok)
         for bound in bounds:
             first = jnp.maximum(first, jnp.where(bound <= middle, bound, 0))
             last = jnp.minimum(last, jnp.where(bound > middle, bound, n * tok))
-        low_owns = last - middle <= middle - first
-        return jnp.where(low_owns, middle, first), jnp.where(low_owns, last, middle)
+        below, above = middle - first, last - middle
+        mode = jnp.int32(0)
+        for count in range(1, CHUNK + 1):
+            fits = below <= slots[count]
+            if count < CHUNK:
+                fits = fits & (above <= slots[CHUNK - count])
+            mode = jnp.where(fits, count, mode)
+        return first, last, mode
 
     token_start = side * group_tokens
-    high_edge = edges(token_start)[1]
-    low_edge = edges(token_start + group_tokens)[0]
-
-    def clear(begin, end):
-        @pl.loop(0, heads)
-        def _(head):
-            recv[head, :, begin:end, :] = jnp.zeros((4, end - begin, HEAD_DIM), jnp.bfloat16)
-
-    if padded > window:
-        clear(window, padded)
-
-    @pl.when(side == 0)
-    def _():
-        clear(0, halo)
-
-    @pl.when(side == GROUPS - 1)
-    def _():
-        clear(group_end, window)
-
-    def segment(shape, dim, start):
+    straddles = straddle(token_start), straddle(token_start + group_tokens)
+
+    def clear(index, begin, end):
+        @pl.loop(0, chunks)
+        def _(chunk):
+            recv[chunk * CHUNK + index, :, begin:end, :] = jnp.zeros(
+                (4, end - begin, HEAD_DIM), jnp.bfloat16
+            )
+
+    for index in range(CHUNK):
+        above = own_end[index] + slots[CHUNK - index]
+        if padded > above:
+            clear(index, above, padded)
+
+        @pl.when(side == 0)
+        def _():
+            clear(index, 0, low[index])
+
+        @pl.when(side == GROUPS - 1)
+        def _():
+            clear(index, own_end[index], above)
+
+    def segment(shape, dim, start, shift):
         inside = lax.broadcasted_iota(jnp.int32, shape, dim) + start
-        places = inside + (token_start - halo)
+        places = inside + (token_start - shift)
         found = jnp.zeros(shape, jnp.int32)
         for bound in bounds:
             found = found + (places >= bound).astype(jnp.int32)
         valid = (inside < window) & (places >= 0) & (places < n * tok)
         return jnp.where(valid, found, -1)
 
-    group_rows = ((halo, halo + halo), (group_end - halo, group_end))
-    halo_rows = ((0, halo), (group_end, window))
-
-    def relay(head):
-        arrived = recv.at[head, :, pl.ds(0, (members - 1) * tok), :]
-        pltpu.make_async_copy(arrived, arrived, in_recv.at[head]).wait()
-        own = recv.at[head, pl.ds(2, 2), pl.ds(0, tok), :]
-        pltpu.make_async_copy(own, own, own_sem.at[head]).wait()
+    def taken(upward):
+        table = []
+        for mode in range(CHUNK + 1):
+            if upward:
+                size = slots[mode] if mode else 0
+                table.append([(index, index * size, size) for index in range(mode)])
+            else:
+                size = slots[CHUNK - mode] if mode < CHUNK else 0
+                table.append([(index, (index - mode) * size, size) for index in range(mode, CHUNK)])
+        return table
+
+    def place_of(upward, halo, index, size):
+        if upward:
+            return (low[index] if halo else own_end[index]) - size
+        return own_end[index] if halo else low[index]
+
+    def modes(which):
+        held = jnp.full((TILE, HEAD_DIM), straddles[which][2], jnp.int32)
+        return [held == mode for mode in range(CHUNK + 1)]
+
+    def gather(target, source, which, upward, halo, chunk):
+        masks = modes(which)
+
+        @pl.loop(0, 4)
+        def _(place):
+            for begin in range(0, capacity, TILE):
+                value = None
+                for mode, table in enumerate(taken(upward)):
+                    for index, start, size in table:
+                        if start <= begin < start + size:
+                            row = place_of(upward, halo, index, size) + begin - start
+                            found = source[chunk * CHUNK + index, place, row:row + TILE, :]
+                            value = found if value is None else jnp.where(masks[mode], found, value)
+                if value is None:
+                    value = jnp.zeros((TILE, HEAD_DIM), jnp.bfloat16)
+                target[chunk, which, place, begin:begin + TILE, :] = value
+
+    def scatter(source, target, which, upward, halo, chunk):
+        masks = modes(which)
+        first, last, mode_now = straddles[which]
+        lane_rows = lax.broadcasted_iota(jnp.int32, (TILE, HEAD_DIM), 0)
+        limits = []
+        for mode in range(CHUNK + 1):
+            if upward:
+                limits.append(jnp.where(mode_now == mode, first, n * tok))
+            else:
+                limits.append(jnp.where(mode_now == mode, last, -1))
+
+        @pl.loop(0, 4)
+        def _(place):
+            for index in range(CHUNK):
+                span = slots[index + 1] if upward else slots[CHUNK - index]
+                base = place_of(upward, halo, index, span)
+                for row in range(base, base + span, TILE):
+                    value = None if halo else target[chunk * CHUNK + index, place, row:row + TILE, :]
+                    tokens = lane_rows + (token_start + row - low[index])
+                    for mode, table in enumerate(taken(upward)):
+                        for owner, start, size in table:
+                            begin = place_of(upward, halo, owner, size)
+                            if owner == index and begin <= row < begin + size:
+                                offset = start + row - begin
+                                found = source[chunk, which, place, offset:offset + TILE, :]
+                                if halo:
+                                    mask = masks[mode]
+                                elif upward:
+                                    mask = tokens >= limits[mode]
+                                else:
+                                    mask = tokens < limits[mode]
+                                value = found if value is None else jnp.where(mask, found, value)
+                    target[chunk * CHUNK + index, place, row:row + TILE, :] = value
+
+    def relay(chunk):
+        for index in range(CHUNK):
+            head = chunk * CHUNK + index
+            arrived = recv.at[head, :, pl.ds(0, (members - 1) * tok), :]
+            pltpu.make_async_copy(arrived, arrived, in_recv.at[head]).wait()
+            own = recv.at[head, pl.ds(2, 2), pl.ds(0, tok), :]
+            pltpu.make_async_copy(own, own, own_sem.at[head]).wait()
 
         def act(which, group):
-            source, target = group_rows[which], halo_rows[1 - which]
+            gather(give, recv, which, which == 1, False, chunk)
             remote(
-                recv.at[head, :, source[0]:source[1], :], recv.at[head, :, target[0]:target[1], :],
-                halo_send.at[which, head], halo_recv.at[1 - which, head], device(group, place_in),
+                give.at[chunk, which], take.at[chunk, 1 - which],
+                halo_send.at[which, chunk], halo_recv.at[1 - which, chunk], device(group, place_in),
             ).start()
 
         each_side(act)
 
-    def attend(head):
+    def attend(chunk):
         def arrive(which, group):
-            target = halo_rows[which]
-            held = recv.at[head, :, target[0]:target[1], :]
-            pltpu.make_async_copy(held, held, halo_recv.at[which, head]).wait()
+            held = take.at[chunk, which]
+            pltpu.make_async_copy(held, held, halo_recv.at[which, chunk]).wait()
+            scatter(take, recv, which, which == 0, True, chunk)
 
         each_side(arrive)
+
+        @pl.loop(0, CHUNK)
+        def _(index):
+            shift = jnp.int32(low[0])
+            for other in range(1, CHUNK):
+                shift = jnp.where(index == other, low[other], shift)
+            attend_head(chunk * CHUNK + index, shift)
+
+        def act(which, group):
+            gather(give_back, back, which, which == 0, True, chunk)
+            remote(
+                give_back.at[chunk, which], take_back.at[chunk, 1 - which],
+                beside_send.at[which, chunk], beside_recv.at[1 - which, chunk],
+                device(group, place_in),
+            ).start()
+
+        each_side(act)
+
+    def attend_head(head, shift):
         key_acc[...] = jnp.zeros_like(key_acc)
         value_acc[...] = jnp.zeros_like(value_acc)
         for start in range(0, window, QUERY_BLOCK):
             block = min(QUERY_BLOCK, window - start)
-            low = max(0, start - reach) // LANES * LANES
-            high = min(padded, -(-(start + block + reach) // LANES) * LANES)
+            first = max(0, start - reach) // LANES * LANES
+            last = min(padded, -(-(start + block + reach) // LANES) * LANES)
             query = recv[head, 0, start:start + block, :]
-            keys = recv[head, 1, low:high, :]
-            value_rows = recv[head, 2, low:high, :]
+            keys = recv[head, 1, first:last, :]
+            value_rows = recv[head, 2, first:last, :]
             cot = recv[head, 3, start:start + block, :]
-            live = segment((block, 1), 0, start) == segment((1, high - low), 1, low)
+            live = segment((block, 1), 0, start, shift) == segment((1, last - first), 1, first, shift)
             scores = jnp.where(live, dot(query, keys, 1, 1), -1e30)
             highest = jnp.max(scores, axis=1, keepdims=True)
             expon = jnp.exp((scores - highest) * scale)
@@ -250,55 +375,39 @@
             dscore = (probs * (dprob - delta) * scale).astype(jnp.bfloat16)
             back[head, 0, start:start + block, :] = context
             back[head, 1, start:start + block, :] = dot(dscore, keys, 1, 0).astype(jnp.bfloat16)
-            key_acc[low:high, :] += dot(dscore, query, 0, 0)
-            value_acc[low:high, :] += dot(half, cot, 0, 0)
+            key_acc[first:last, :] += dot(dscore, query, 0, 0)
+            value_acc[first:last, :] += dot(half, cot, 0, 0)
         back[head, 2] = key_acc[0:window, :].astype(jnp.bfloat16)
         back[head, 3] = value_acc[0:window, :].astype(jnp.bfloat16)
 
-        def act(which, group):
-            source = halo_rows[which]
-            remote(
-                back.at[head, :, source[0]:source[1], :], beside.at[head, 1 - which],
-                beside_send.at[which, head], beside_recv.at[1 - which, head],
-                device(group, place_in),
-            ).start()
-
-        each_side(act)
-
-    def distribute(head):
+    def distribute(chunk):
         def merge(which, group):
-            held = beside.at[head, which]
-            pltpu.make_async_copy(held, held, beside_recv.at[which, head]).wait()
-            begin, end = group_rows[which]
-            places = lax.broadcasted_iota(jnp.int32, (halo, HEAD_DIM), 0) + (
-                token_start + begin - halo
-            )
-            outside = (places >= low_edge) if which else (places < high_edge)
-            for place in range(4):
-                back[head, place, begin:end, :] = jnp.where(
-                    outside, beside[head, which, place], back[head, place, begin:end, :]
-                )
+            held = take_back.at[chunk, which]
+            pltpu.make_async_copy(held, held, beside_recv.at[which, chunk]).wait()
+            scatter(take_back, back, which, which == 1, False, chunk)
 
         each_side(merge)
-        cols = columns(place_in, head)
-
-        @pl.loop(1, members)
-        def _(step):
-            other = member(step)
-            remote(
-                back.at[head, :, rows(other), :], out_ref.at[:, :, cols],
-                out_send.at[head], out_recv.at[head], device(side, other),
-            ).start()
-
-        out_ref[:, :, cols] = back[head, :, rows(place_in), :]
-
-    @pl.loop(0, heads + ATTEND_LAG + DISTRIBUTE_LAG)
+        for index in range(CHUNK):
+            head = chunk * CHUNK + index
+            cols = columns(place_in, head)
+
+            @pl.loop(1, members)
+            def _(step):
+                other = member(step)
+                remote(
+                    back.at[head, :, rows(other, index), :], out_ref.at[:, :, cols],
+                    out_send.at[head], out_recv.at[head], device(side, other),
+                ).start()
+
+            out_ref[:, :, cols] = back[head, :, rows(place_in, index), :]
+
+    @pl.loop(0, chunks + ATTEND_LAG + DISTRIBUTE_LAG)
     def _(step):
-        @pl.when(step < heads)
+        @pl.when(step < chunks)
         def _():
             relay(step)
 
-        @pl.when((step >= ATTEND_LAG) & (step < heads + ATTEND_LAG))
+        @pl.when((step >= ATTEND_LAG) & (step < chunks + ATTEND_LAG))
         def _():
             attend(step - ATTEND_LAG)
 
@@ -388,10 +497,12 @@
         pltpu.make_async_copy(moved, moved, in_send.at[head]).wait()
         pltpu.make_async_copy(moved, moved, out_send.at[head]).wait()
 
+    @pl.loop(0, chunks)
+    def _(chunk):
         def drain(which, group):
-            held = beside.at[head, which]
-            pltpu.make_async_copy(held, held, halo_send.at[which, head]).wait()
-            pltpu.make_async_copy(held, held, beside_send.at[which, head]).wait()
+            held = give.at[chunk, which]
+            pltpu.make_async_copy(held, held, halo_send.at[which, chunk]).wait()
+            pltpu.make_async_copy(held, held, beside_send.at[which, chunk]).wait()
 
         each_side(drain)
 
@@ -404,11 +515,13 @@
     heads = GROUPS * shared
     tokens = n * tok
     reach = tokens // 3 - 1
-    halo = -(-((reach + 1) // 2) // 16) * 16
-    window = tokens // GROUPS + 2 * halo
+    group_tokens = tokens // GROUPS
+    chunks = heads // CHUNK
+    capacity, slots = slot_sizes(reach + 1, group_tokens, CHUNK)
+    window = group_tokens + max(slots[i + 1] + slots[CHUNK - i] for i in range(CHUNK))
     padded = -(-window // LANES) * LANES
     cosine, sine = rope_tables(positions[0], HEAD_DIM)
-    sizes = (n, replicas, heads, tok, lengths.shape[1], reach, halo, padded)
+    sizes = (n, replicas, heads, tok, lengths.shape[1], reach, capacity, slots, window, padded)
     vmem = pl.BlockSpec(memory_space=pltpu.VMEM)
     hbm = pl.BlockSpec(memory_space=pl.ANY)
     gain_rows = (2 * shared, LANES)
@@ -424,7 +537,10 @@
         ],
         out_specs=(vmem, vmem),
         scratch_shapes=[
-            pltpu.VMEM((heads, 2, 4, halo, HEAD_DIM), half),
+            pltpu.VMEM((chunks, 2, 4, capacity, HEAD_DIM), half),
+            pltpu.VMEM((chunks, 2, 4, capacity, HEAD_DIM), half),
+            pltpu.VMEM((chunks, 2, 4, capacity, HEAD_DIM), half),
+            pltpu.VMEM((chunks, 2, 4, capacity, HEAD_DIM), half),
             pltpu.VMEM((heads, n // GROUPS, 2, tok, HEAD_DIM), half),
             pltpu.VMEM((heads, 4, padded, HEAD_DIM), half),
             pltpu.VMEM((heads, 4, window, HEAD_DIM), half),
@@ -444,10 +560,10 @@
             pltpu.SemaphoreType.DMA((heads,)),
             pltpu.SemaphoreType.DMA((3,)),
             pltpu.SemaphoreType.DMA((3,)),
-            pltpu.SemaphoreType.DMA((2, heads)),
-            pltpu.SemaphoreType.DMA((2, heads)),
-            pltpu.SemaphoreType.DMA((2, heads)),
-            pltpu.SemaphoreType.DMA((2, heads)),
+            pltpu.SemaphoreType.DMA((2, chunks)),
+            pltpu.SemaphoreType.DMA((2, chunks)),
+            pltpu.SemaphoreType.DMA((2, chunks)),
+            pltpu.SemaphoreType.DMA((2, chunks)),
         ],
         compiler_params=pltpu.CompilerParams(
             collective_id=0, has_side_effects=True, vmem_limit_bytes=56 * 1024 * 1024

time: 165 us -> 134 us (0.81)
  Pallas kernels: 157 us -> 126 us
    pallas_call x1, Pallas kernels: 157 us -> 126 us  [on_device(): pl.pallas_call(functools.partial(kernel, sizes), out_shape=(jax.ShapeDtyp...]
where the time goes in v1:
time: 134 us
  Pallas kernels  126 us (94%)
  local copies, waits for them, and re-layouts  4.95 us (4%)
  other arithmetic  2.39 us (2%)
    pallas_call x1, Pallas kernels, on_device(): pl.pallas_call(functools.partial(kernel, sizes), out_shape=(jax.ShapeDtyp...  126 us
    slice x1, local copies, waits for them, and re-layouts, on_device(): outs[3][None]  4.28 us

profile of v1, /device:TPU:0, one launch (start us, length us, event | category | flops | bytes accessed | tf_op | source)
XLA Modules:
  0.0 133.8 jit_solution(16056226809927408020)
XLA Ops:
  0.6 0.7 convert_element_type.4
  1.3 1.7 %sine_multiply_fusion = (f32[128,128]{1,0:T(8,128)}, f32[128,128]{1,0:T(8,128)}) fusion(f32[128]{0:T(128)} %constant.11.clone, f32[128]{0:T(128)} %constant.10.clone, f32[128]{0:T(128)S(1)} %get-tuple-element.19, f32[128]{0:T(128)S(1)} %get-tuple-element.20, f32[128]{0:T(128)S(1)} %get-tuple-element.18, pred[128]{0:T(512)(128)(4,1)} %constant.8.clone, ...), kind=kLoop, calls=%fused_computation | loop fusion | flops 65536 | bytes 133888 | tf_op jit(solution)/shard_map/mul | solution.py:36
  3.0 125.8 %shard_map.163 = (bf16[4,128,4096]{2,1,0:T(8,128)(2,1)}, f32[8,8,128]{2,1,0:T(8,128)}) custom-call(s32[1,6]{1,0:T(1,128)} %len_ref.1, bf16[128,4096]{1,0:T(8,128)(2,1)} %bitcast.14, bf16[128,4096]{1,0:T(8,128)(2,1)} %bitcast.15, bf16[128,4096]{1,0:T(8,128)(2,1)} %bitcast.16, bf16[128,4096]{1,0:T(8,128)(2,1)} %bitcast.17, f32[1,4096]{1,0:T(1,128)} %bitcast.18, ...), custom_call_target="tpu_custom_call" | custom-call | tf_op jit(solution)/shard_map/pallas_call | solution.py:529
  128.9 0.0 copy-start
  128.9 4.3 %fusion.1 = (bf16[1,128,4096]{2,1,0:T(8,128)(2,1)}, bf16[1,128,4096]{2,1,0:T(8,128)(2,1)}, bf16[1,128,4096]{2,1,0:T(8,128)(2,1)}, bf16[1,128,4096]{2,1,0:T(8,128)(2,1)}) fusion(bf16[4,128,4096]{2,1,0:T(8,128)(2,1)} %get-tuple-element.8), kind=kLoop, calls=%fused_computation.6 | loop fusion | bytes 8388608 | tf_op jit(solution)/shard_map/slice | solution.py:577
  133.2 0.0 copy-done
  133.2 0.6 fusion.2
  (2 shorter events, 0.0 us)
Async XLA Ops:
  128.9 4.3 %copy-start = (f32[8,8,128]{2,1,0:T(8,128)S(1)}, f32[8,8,128]{2,1,0:T(8,128)}, u32[]{:S(2)}) copy-start(f32[8,8,128]{2,1,0:T(8,128)} %get-tuple-element.9) | copy-start | bytes 98308

commit v2 on v1

--- a/solution.py
+++ b/solution.py
@@ -15,12 +15,15 @@
 CHUNK = 2
 TILE = 16
 ATTEND_LAG = 2
-DISTRIBUTE_LAG = 1
+DISTRIBUTE_LAG = 2
+NORM_LAG = 1
+DEFERRED = 2
+AHEAD = 1
 EPSILON = 1e-06
 MESH = pl.DeviceIdType.MESH
 
 
-def rope_tables(position_rows, head_dim):
+def rope_constants(head_dim):
     half = head_dim // 2
     sixth = head_dim // 6
     first = half - 2 * sixth
@@ -29,11 +32,7 @@
     begin = np.where(section == 0, 0, np.where(section == 1, first, first + sixth))
     number = np.where(section == 0, first, sixth)
     freqs = (10000.0 ** (-(pairs - begin) / number)).astype(np.float32)
-    sign = np.where(np.arange(head_dim) < half, -1.0, 1.0).astype(np.float32)
-    rows = position_rows.astype(jnp.float32)[:, :, None]
-    chosen = jnp.where(section == 0, rows[0], jnp.where(section == 1, rows[1], rows[2]))
-    angle = chosen * freqs
-    return jnp.cos(angle), jnp.sin(angle) * sign
+    return (section == np.arange(3)[:, None]).astype(np.float32) * freqs
 
 
 def slot_sizes(longest, group_tokens, chunk):
@@ -61,11 +60,13 @@
 
 def kernel(
     sizes,
-    len_ref, q_ref, k_ref, v_ref, do_ref, gq_ref, gk_ref, cos_ref, sin_ref,
-    out_ref, gain_ref,
+    len_ref, q_hbm, k_hbm, v_ref, do_ref, gq_ref, gk_ref, pos_ref, freq_ref,
+    att_ref, dq_ref, dk_ref, dv_ref, gain_ref,
+    q_ref, k_ref, cos_ref, sin_ref, inner_q, inner_k,
     give, take, give_back, take_back, sent, recv, back, key_acc, value_acc, scale_q, scale_k,
     part, seq_part, dp_sum, dp_part, total,
-    in_send, in_recv, own_sem, out_send, out_recv, gain_send, gain_recv,
+    raw_sem, in_send, in_recv, own_sem, out_send, out_recv, late_send, late_recv,
+    gain_send, gain_recv,
     halo_send, halo_recv, beside_send, beside_recv,
 ):
     n, replicas, heads, tok, clips, reach, capacity, slots, window, padded = sizes
@@ -113,6 +114,13 @@
             device_id=device, device_id_type=MESH,
         )
 
+    loads = [
+        pltpu.make_async_copy(q_hbm, q_ref, raw_sem.at[0]),
+        pltpu.make_async_copy(k_hbm, k_ref, raw_sem.at[1]),
+    ]
+    for load in loads:
+        load.start()
+
     barrier = pltpu.get_barrier_semaphore()
     for step in range(1, n):
         pl.semaphore_signal(barrier, inc=1, device_id=(my_dp, peer(step)), device_id_type=MESH)
@@ -137,8 +145,21 @@
                     in_send.at[head], in_recv.at[head], device(side, other),
                 ).start()
 
-    for index in range(CHUNK):
-        send_values(index, index)
+    ahead = min(AHEAD, chunks)
+    for head in range(ahead * CHUNK):
+        send_values(head, head % CHUNK)
+
+    held = jnp.concatenate([pos_ref[axis] for axis in range(3)], axis=0)
+    angle = lax.dot_general(
+        held.astype(jnp.float32), freq_ref[...], (((0,), (0,)), ((), ())),
+        precision=lax.Precision.HIGHEST, preferred_element_type=jnp.float32,
+    )
+    negative = lax.broadcasted_iota(jnp.int32, (tok, HEAD_DIM), 1) < HEAD_DIM // 2
+    cos_ref[...] = jnp.cos(angle)
+    sine = jnp.sin(angle)
+    sin_ref[...] = jnp.where(negative, -sine, sine)
+    for load in loads:
+        load.wait()
 
     def squares(index, sums):
         cols = pl.ds(pl.multiple_of(index * LANES, LANES), LANES)
@@ -159,11 +180,6 @@
 
     @pl.loop(0, chunks)
     def _(chunk):
-        @pl.when(chunk > 0)
-        def _():
-            for index in range(CHUNK):
-                send_values(chunk * CHUNK + index, index)
-
         for index in range(CHUNK):
             head = chunk * CHUNK + index
 
@@ -183,6 +199,11 @@
                 ((q_ref, gq_ref, scale_q), (k_ref, gk_ref, scale_k))
             ):
                 recv[head, place, rows(place_in, index), :] = rotated(ref, gain, norm, cols)
+
+        @pl.when(chunk + ahead < chunks)
+        def _():
+            for index in range(CHUNK):
+                send_values((chunk + ahead) * CHUNK + index, index)
 
     bounds = []
     running = len_ref[0, 0]
@@ -373,11 +394,11 @@
             )
             dprob = dot(cot, value_rows, 1, 1)
             dscore = (probs * (dprob - delta) * scale).astype(jnp.bfloat16)
-            back[head, 0, start:start + block, :] = context
-            back[head, 1, start:start + block, :] = dot(dscore, keys, 1, 0).astype(jnp.bfloat16)
+            back[head, 2, start:start + block, :] = context
+            back[head, 0, start:start + block, :] = dot(dscore, keys, 1, 0).astype(jnp.bfloat16)
             key_acc[first:last, :] += dot(dscore, query, 0, 0)
             value_acc[first:last, :] += dot(half, cot, 0, 0)
-        back[head, 2] = key_acc[0:window, :].astype(jnp.bfloat16)
+        back[head, 1] = key_acc[0:window, :].astype(jnp.bfloat16)
         back[head, 3] = value_acc[0:window, :].astype(jnp.bfloat16)
 
     def distribute(chunk):
@@ -387,6 +408,13 @@
             scatter(take_back, back, which, which == 1, False, chunk)
 
         each_side(merge)
+        outward(chunk, 0, (dq_ref, dk_ref), out_send, out_recv)
+
+        @pl.when(chunk < chunks - DEFERRED)
+        def _():
+            outward(chunk, 2, (att_ref, dv_ref), late_send, late_recv)
+
+    def outward(chunk, first, targets, send, receive):
         for index in range(CHUNK):
             head = chunk * CHUNK + index
             cols = columns(place_in, head)
@@ -394,14 +422,48 @@
             @pl.loop(1, members)
             def _(step):
                 other = member(step)
-                remote(
-                    back.at[head, :, rows(other, index), :], out_ref.at[:, :, cols],
-                    out_send.at[head], out_recv.at[head], device(side, other),
-                ).start()
-
-            out_ref[:, :, cols] = back[head, :, rows(place_in, index), :]
-
-    @pl.loop(0, chunks + ATTEND_LAG + DISTRIBUTE_LAG)
+                for place, target in enumerate(targets):
+                    remote(
+                        back.at[head, first + place, rows(other, index), :], target.at[:, cols],
+                        send.at[head], receive.at[head], device(side, other),
+                    ).start()
+
+            for place, target in enumerate(targets):
+                target[:, cols] = back[head, first + place, rows(place_in, index), :]
+
+    def arrived_pair(head, sem):
+        held = recv.at[head, 0:2, pl.ds(0, (members - 1) * tok), :]
+        pltpu.make_async_copy(held, held, sem.at[head]).wait()
+
+    def turned_back(grad, ref, norm, cols):
+        grads = grad[:, cols].astype(jnp.float32)
+        turned = grads * cos_ref[...] - pltpu.roll(grads, HEAD_DIM // 2, 1) * sin_ref[...]
+        return turned, ref[:, cols].astype(jnp.float32) * norm[...]
+
+    sides = (
+        (dq_ref, q_ref, gq_ref, scale_q, inner_q), (dk_ref, k_ref, gk_ref, scale_k, inner_k),
+    )
+    inner_q[...] = zero
+    inner_k[...] = zero
+
+    def first_pass(chunk):
+        for index in range(CHUNK):
+            head = chunk * CHUNK + index
+            arrived_pair(head, out_recv)
+
+            @pl.loop(0, members)
+            def _(owner):
+                cols = columns(owner, head)
+                for place, (grad, ref, gain, norm, inner) in enumerate(sides):
+                    turned, hat = turned_back(grad, ref, norm, cols)
+                    both = turned * hat
+                    row = place * shared + lax.rem(head, shared)
+                    part[owner * ratio + head // shared, pl.ds(row, 1), :] = jnp.sum(
+                        both, axis=0, keepdims=True
+                    )
+                    inner[...] += both * gain[:, cols]
+
+    @pl.loop(0, chunks + ATTEND_LAG + DISTRIBUTE_LAG + NORM_LAG)
     def _(step):
         @pl.when(step < chunks)
         def _():
@@ -411,91 +473,82 @@
         def _():
             attend(step - ATTEND_LAG)
 
-        @pl.when(step >= ATTEND_LAG + DISTRIBUTE_LAG)
+        @pl.when(
+            (step >= ATTEND_LAG + DISTRIBUTE_LAG) & (step < chunks + ATTEND_LAG + DISTRIBUTE_LAG)
+        )
         def _():
             distribute(step - ATTEND_LAG - DISTRIBUTE_LAG)
 
-    def turned_back(place, ref, norm, cols):
-        grads = out_ref[place, :, cols].astype(jnp.float32)
-        turned = grads * cos_ref[...] - pltpu.roll(grads, HEAD_DIM // 2, 1) * sin_ref[...]
-        return turned, ref[:, cols].astype(jnp.float32) * norm[...]
-
-    inner = (zero, zero)
-    for head in range(heads):
-        arrived = out_ref.at[:, :, pl.ds(0, (members - 1) * HEAD_DIM)]
-        pltpu.make_async_copy(arrived, arrived, out_recv.at[head]).wait()
-
-        def first_pass(owner, sums):
-            cols = columns(owner, head)
-            results = []
-            for place, (ref, gain, norm) in enumerate(
-                ((q_ref, gq_ref, scale_q), (k_ref, gk_ref, scale_k))
-            ):
-                turned, hat = turned_back(place + 1, ref, norm, cols)
-                both = turned * hat
-                row = place * shared + head % shared
-                part[owner * ratio + head // shared, row:row + 1, :] = jnp.sum(both, axis=0, keepdims=True)
-                results.append(sums[place] + both * gain[:, cols])
-            return tuple(results)
-
-        inner = lax.fori_loop(0, members, first_pass, inner)
+        @pl.when(step >= ATTEND_LAG + DISTRIBUTE_LAG + NORM_LAG)
+        def _():
+            first_pass(step - ATTEND_LAG - DISTRIBUTE_LAG - NORM_LAG)
+
+    per = n // replicas
+
+    def portion(index):
+        return pl.ds(index * per, per)
+
+    for step in range(1, replicas):
+        other = lax.rem(my_dp + step, replicas)
+        remote(
+            part.at[portion(other)], dp_part.at[my_dp], gain_send.at[0], gain_recv.at[0], (other, me)
+        ).start()
+    dp_part[my_dp] = part[portion(my_dp)]
+
+    @pl.loop(chunks - min(DEFERRED, chunks), chunks)
+    def _(chunk):
+        outward(chunk, 2, (att_ref, dv_ref), late_send, late_recv)
+
+    means = [
+        jnp.broadcast_to(jnp.sum(inner[...], axis=1, keepdims=True) / feature, (tok, LANES))
+        for inner in (inner_q, inner_k)
+    ]
+
+    def second_pass(index):
+        cols = pl.ds(pl.multiple_of(index * LANES, LANES), LANES)
+        for (grad, ref, gain, norm, _), mean in zip(sides, means):
+            turned, hat = turned_back(grad, ref, norm, cols)
+            result = norm[...] * (turned * gain[:, cols] - hat * mean)
+            grad[:, cols] = result.astype(jnp.bfloat16)
+
+    pl.loop(0, feature // LANES)(second_pass)
+
+    def wait_all(ref, count, sem):
+        held = ref.at[pl.ds(0, count)]
+        pltpu.make_async_copy(held, held, sem).wait()
+
+    wait_all(dp_part, replicas - 1, gain_recv.at[0])
+    dp_sum[...] = jnp.sum(dp_part[...], axis=0)
 
     @pl.loop(1, n)
     def _(step):
         other = peer(step)
         remote(
-            part.at[other], seq_part.at[me], gain_send.at[0], gain_recv.at[0], (my_dp, other)
+            dp_sum, seq_part.at[me], gain_send.at[1], gain_recv.at[1], (my_dp, other)
         ).start()
 
-    seq_part[me] = part[me]
-    inner_q, inner_k = (
-        jnp.broadcast_to(jnp.sum(sums, axis=1, keepdims=True) / feature, (tok, LANES))
-        for sums in inner
-    )
-
-    def second_pass(index):
-        cols = pl.ds(pl.multiple_of(index * LANES, LANES), LANES)
-        for place, (ref, gain, norm, mean) in enumerate(
-            ((q_ref, gq_ref, scale_q, inner_q), (k_ref, gk_ref, scale_k, inner_k))
-        ):
-            turned, hat = turned_back(place + 1, ref, norm, cols)
-            result = norm[...] * (turned * gain[:, cols] - hat * mean)
-            out_ref[place + 1, :, cols] = result.astype(jnp.bfloat16)
-
-    pl.loop(0, feature // LANES)(second_pass)
-
-    def wait_all(ref, count, sem):
-        held = ref.at[pl.ds(0, count)]
-        pltpu.make_async_copy(held, held, sem).wait()
-
-    wait_all(seq_part, n - 1, gain_recv.at[0])
-    dp_sum[...] = jnp.sum(seq_part[...], axis=0)
+    seq_part[me] = dp_sum[...]
+    wait_all(seq_part, n - 1, gain_recv.at[1])
+    total[...] = jnp.sum(seq_part[...], axis=0) / replicas
     for step in range(1, replicas):
         other = lax.rem(my_dp + step, replicas)
         remote(
-            dp_sum, dp_part.at[my_dp], gain_send.at[1], gain_recv.at[1], (other, me)
+            total, gain_ref.at[portion(my_dp)], gain_send.at[2], gain_recv.at[2], (other, me)
         ).start()
-    dp_part[my_dp] = dp_sum[...]
-    wait_all(dp_part, replicas - 1, gain_recv.at[1])
-    total[...] = jnp.sum(dp_part[...], axis=0) / replicas
-
-    @pl.loop(1, n)
-    def _(step):
-        other = peer(step)
-        remote(
-            total, gain_ref.at[me], gain_send.at[2], gain_recv.at[2], (my_dp, other)
-        ).start()
-
-    gain_ref[me] = total[...]
-    wait_all(gain_ref, n - 1, gain_recv.at[2])
-
-    wait_all(seq_part, n - 1, gain_send.at[0])
-    wait_all(dp_part, replicas - 1, gain_send.at[1])
-    wait_all(seq_part, n - 1, gain_send.at[2])
-    for head in range(heads):
+    gain_ref[portion(my_dp)] = total[...]
+    wait_all(dp_part, replicas - 1, gain_recv.at[2])
+
+    wait_all(dp_part, replicas - 1, gain_send.at[0])
+    wait_all(seq_part, n - 1, gain_send.at[1])
+    wait_all(dp_part, replicas - 1, gain_send.at[2])
+
+    @pl.loop(0, heads)
+    def _(head):
         moved = recv.at[head, :, pl.ds(0, (members - 1) * tok), :]
         pltpu.make_async_copy(moved, moved, in_send.at[head]).wait()
-        pltpu.make_async_copy(moved, moved, out_send.at[head]).wait()
+        arrived_pair(head, out_send)
+        arrived_pair(head, late_send)
+        arrived_pair(head, late_recv)
 
     @pl.loop(0, chunks)
     def _(chunk):
@@ -505,6 +558,24 @@
             pltpu.make_async_copy(held, held, beside_send.at[which, chunk]).wait()
 
         each_side(drain)
+
+
+def finish(gains_ref, *refs):
+    arrays, targets, (gq_ref, gk_ref), sems = refs[:4], refs[4:8], refs[8:10], refs[10]
+    copies = [
+        pltpu.make_async_copy(source, target, sems.at[index])
+        for index, (source, target) in enumerate(zip(arrays, targets))
+    ]
+    for copy in copies:
+        copy.start()
+    owners, shared = gains_ref.shape[0], gains_ref.shape[1] // 2
+    for owner in range(owners):
+        for row in range(shared):
+            cols = slice((owner * shared + row) * LANES, (owner * shared + row + 1) * LANES)
+            gq_ref[:, cols] = gains_ref[owner, row:row + 1, :]
+            gk_ref[:, cols] = gains_ref[owner, shared + row:shared + row + 1, :]
+    for copy in copies:
+        copy.wait()
 
 
 def on_device(q_raw, k_raw, values, grad_out, q_gain, k_gain, lengths, positions):
@@ -520,23 +591,28 @@
     capacity, slots = slot_sizes(reach + 1, group_tokens, CHUNK)
     window = group_tokens + max(slots[i + 1] + slots[CHUNK - i] for i in range(CHUNK))
     padded = -(-window // LANES) * LANES
-    cosine, sine = rope_tables(positions[0], HEAD_DIM)
     sizes = (n, replicas, heads, tok, lengths.shape[1], reach, capacity, slots, window, padded)
     vmem = pl.BlockSpec(memory_space=pltpu.VMEM)
     hbm = pl.BlockSpec(memory_space=pl.ANY)
     gain_rows = (2 * shared, LANES)
     half, full = jnp.bfloat16, jnp.float32
-    outs, gains = pl.pallas_call(
+    *outs, gains = pl.pallas_call(
         functools.partial(kernel, sizes),
         out_shape=(
-            jax.ShapeDtypeStruct((4, tok, feature), half),
-            jax.ShapeDtypeStruct((n,) + gain_rows, full),
+            *[pltpu.VMEM((tok, feature), half)] * 4,
+            pltpu.VMEM((n,) + gain_rows, full),
         ),
         in_specs=[
-            pl.BlockSpec(memory_space=pltpu.SMEM), vmem, vmem, hbm, hbm, vmem, vmem, vmem, vmem,
+            pl.BlockSpec(memory_space=pltpu.SMEM), hbm, hbm, hbm, hbm, vmem, vmem, vmem, vmem,
         ],
-        out_specs=(vmem, vmem),
+        out_specs=(vmem,) * 5,
         scratch_shapes=[
+            pltpu.VMEM((tok, feature), half),
+            pltpu.VMEM((tok, feature), half),
+            pltpu.VMEM((tok, HEAD_DIM), full),
+            pltpu.VMEM((tok, HEAD_DIM), full),
+            pltpu.VMEM((tok, LANES), full),
+            pltpu.VMEM((tok, LANES), full),
             pltpu.VMEM((chunks, 2, 4, capacity, HEAD_DIM), half),
             pltpu.VMEM((chunks, 2, 4, capacity, HEAD_DIM), half),
             pltpu.VMEM((chunks, 2, 4, capacity, HEAD_DIM), half),
@@ -549,10 +625,13 @@
             pltpu.VMEM((tok, LANES), full),
             pltpu.VMEM((tok, LANES), full),
             pltpu.VMEM((n,) + gain_rows, full),
-            pltpu.VMEM((n,) + gain_rows, full),
-            pltpu.VMEM(gain_rows, full),
-            pltpu.VMEM((replicas,) + gain_rows, full),
-            pltpu.VMEM(gain_rows, full),
+            pltpu.VMEM((n, n // replicas) + gain_rows, full),
+            pltpu.VMEM((n // replicas,) + gain_rows, full),
+            pltpu.VMEM((replicas, n // replicas) + gain_rows, full),
+            pltpu.VMEM((n // replicas,) + gain_rows, full),
+            pltpu.SemaphoreType.DMA((2,)),
+            pltpu.SemaphoreType.DMA((heads,)),
+            pltpu.SemaphoreType.DMA((heads,)),
             pltpu.SemaphoreType.DMA((heads,)),
             pltpu.SemaphoreType.DMA((heads,)),
             pltpu.SemaphoreType.DMA((heads,)),
@@ -570,12 +649,19 @@
         ),
     )(
         lengths, q_raw[0], k_raw[0], values[0], grad_out[0],
-        q_gain[None], k_gain[None], cosine, sine,
+        q_gain[None], k_gain[None], positions[0][:, None], jnp.asarray(rope_constants(HEAD_DIM)),
     )
-    gains = gains.reshape(n, 2, shared * HEAD_DIM)
+    attended, grad_q, grad_k, grad_v, gain_q, gain_k = pl.pallas_call(
+        finish,
+        out_shape=(jax.ShapeDtypeStruct((tok, feature), half),) * 4
+        + (jax.ShapeDtypeStruct((1, feature), full),) * 2,
+        in_specs=[vmem] * 5,
+        out_specs=(hbm,) * 4 + (vmem,) * 2,
+        scratch_shapes=[pltpu.SemaphoreType.DMA((4,))],
+        compiler_params=pltpu.CompilerParams(vmem_limit_bytes=6 * 1024 * 1024),
+    )(gains, *outs)
     return (
-        outs[0][None], outs[1][None], outs[2][None], outs[3][None],
-        gains[:, 0].reshape(feature), gains[:, 1].reshape(feature),
+        attended[None], grad_q[None], grad_k[None], grad_v[None], gain_q[0], gain_k[0],
     )
 
 

time: 134 us -> 121 us (0.903)
  Pallas kernels: 126 us -> 120 us
  local copies, waits for them, and re-layouts: 4.95 us -> 0 us
  other arithmetic: 2.39 us -> 0 us
    pallas_call x1 -> x2, Pallas kernels: 126 us -> 120 us  [the longest x1 118 us: on_device(): pl.pallas_call(functools.partial(kernel, sizes), out_shape=(*[pltpu.VMEM(...]
    slice x2 -> x0, local copies, waits for them, and re-layouts: 4.92 us -> none  [the longest x1 4.28 us: on_device(): outs[3][None]]
    mul x1 -> x0, other arithmetic: 1.71 us -> none  [rope_tables(): return (jnp.cos(angle), jnp.sin(angle) * sign)]
where the time goes in v2:
time: 121 us
  Pallas kernels  120 us (99%)
    pallas_call x1, Pallas kernels, on_device(): pl.pallas_call(functools.partial(kernel, sizes), out_shape=(*[pltpu.VMEM(...  118 us
    pallas_call x1, Pallas kernels, on_device(): pl.pallas_call(finish, out_shape=(jax.ShapeDtypeStruct((tok, feature), ha...  2.65 us

profile of v2, /device:TPU:0, one launch (start us, length us, event | category | flops | bytes accessed | tf_op | source)
XLA Modules:
  0.0 121.1 jit_solution(7973199144654751132)
XLA Ops:
  0.6 117.8 %shard_map.136 = (bf16[128,4096]{1,0:T(8,128)(2,1)S(1)}, bf16[128,4096]{1,0:T(8,128)(2,1)S(1)}, bf16[128,4096]{1,0:T(8,128)(2,1)S(1)}, bf16[128,4096]{1,0:T(8,128)(2,1)S(1)}, f32[8,8,128]{2,1,0:T(8,128)S(1)}) custom-call(s32[1,6]{1,0:T(1,128)} %len_ref.1, bf16[128,4096]{1,0:T(8,128)(2,1)} %bitcast.13, bf16[128,4096]{1,0:T(8,128)(2,1)} %bitcast.14, ...), custom_call_target="tpu_custom_call" | custom-call | tf_op jit(solution)/shard_map/pallas_call | solution.py:599
  118.5 2.7 %shard_map.137 = (bf16[128,4096]{1,0:T(8,128)(2,1)}, bf16[128,4096]{1,0:T(8,128)(2,1)}, bf16[128,4096]{1,0:T(8,128)(2,1)}, bf16[128,4096]{1,0:T(8,128)(2,1)}, f32[1,4096]{1,0:T(1,128)}, /*index=5*/f32[1,4096]{1,0:T(1,128)}) custom-call(f32[8,8,128]{2,1,0:T(8,128)S(1)} %get-tuple-element.17.gains_ref, bf16[128,4096]{1,0:T(8,128)(2,1)S(1)} %get-tuple-element.18.refs_0_, ...), custom_call_target="tpu_custom_call" | custom-call | tf_op jit(solution)/shard_map/pallas_call | solution.py:654

commit v3 on v2

--- a/solution.py
+++ b/solution.py
@@ -122,12 +122,17 @@
         load.start()
 
     barrier = pltpu.get_barrier_semaphore()
-    for step in range(1, n):
-        pl.semaphore_signal(barrier, inc=1, device_id=(my_dp, peer(step)), device_id_type=MESH)
+
+    def greet(target):
+        pl.semaphore_signal(barrier, inc=1, device_id=target, device_id_type=MESH)
+
+    for step in range(1, members):
+        greet(device(side, member(step)))
     for step in range(1, replicas):
-        other = lax.rem(my_dp + step, replicas)
-        pl.semaphore_signal(barrier, inc=1, device_id=(other, me), device_id_type=MESH)
-    pl.semaphore_wait(barrier, n - 1 + replicas - 1)
+        greet((lax.rem(my_dp + step, replicas), me))
+    each_side(lambda which, group: greet(device(group, place_in)))
+    sides_here = jnp.minimum(side, 1) + jnp.minimum(GROUPS - 1 - side, 1)
+    pl.semaphore_wait(barrier, members - 1 + replicas - 1 + sides_here)
 
     def send_values(head, index):
         cols = columns(place_in, head)

time: 121 us -> 122 us (level)
  no operation moved by 1% of the time
where the time goes in v3:
time: 122 us; the launch traced here: 121 us
  Pallas kernels  121 us (99%)
    pallas_call x1, Pallas kernels, on_device(): pl.pallas_call(functools.partial(kernel, sizes), out_shape=(*[pltpu.VMEM(...  118 us
    pallas_call x1, Pallas kernels, on_device(): pl.pallas_call(finish, out_shape=(jax.ShapeDtypeStruct((tok, feature), ha...  2.65 us

profile of v3, /device:TPU:0, one launch (start us, length us, event | category | flops | bytes accessed | tf_op | source)
XLA Modules:
  0.0 121.5 jit_solution(17534104841805492451)
XLA Ops:
  0.6 118.2 %shard_map.136 = (bf16[128,4096]{1,0:T(8,128)(2,1)S(1)}, bf16[128,4096]{1,0:T(8,128)(2,1)S(1)}, bf16[128,4096]{1,0:T(8,128)(2,1)S(1)}, bf16[128,4096]{1,0:T(8,128)(2,1)S(1)}, f32[8,8,128]{2,1,0:T(8,128)S(1)}) custom-call(s32[1,6]{1,0:T(1,128)} %len_ref.1, bf16[128,4096]{1,0:T(8,128)(2,1)} %bitcast.13, bf16[128,4096]{1,0:T(8,128)(2,1)} %bitcast.14, ...), custom_call_target="tpu_custom_call" | custom-call | tf_op jit(solution)/shard_map/pallas_call | solution.py:604
  118.8 2.7 %shard_map.137 = (bf16[128,4096]{1,0:T(8,128)(2,1)}, bf16[128,4096]{1,0:T(8,128)(2,1)}, bf16[128,4096]{1,0:T(8,128)(2,1)}, bf16[128,4096]{1,0:T(8,128)(2,1)}, f32[1,4096]{1,0:T(1,128)}, /*index=5*/f32[1,4096]{1,0:T(1,128)}) custom-call(f32[8,8,128]{2,1,0:T(8,128)S(1)} %get-tuple-element.17.gains_ref, bf16[128,4096]{1,0:T(8,128)(2,1)S(1)} %get-tuple-element.18.refs_0_, ...), custom_call_target="tpu_custom_call" | custom-call | tf_op jit(solution)/shard_map/pallas_call | solution.py:659

commit v4 on v2

--- a/solution.py
+++ b/solution.py
@@ -1,4 +1,5 @@
 import functools
+import random
 
 import jax
 import jax.numpy as jnp
@@ -11,6 +12,8 @@
 HEAD_DIM = 128
 LANES = 128
 QUERY_BLOCK = 256
+WHOLE_SCORES = 1 << 19
+LOG2_E = float(np.log2(np.e))
 GROUPS = 4
 CHUNK = 2
 TILE = 16
@@ -35,21 +38,110 @@
     return (section == np.arange(3)[:, None]).astype(np.float32) * freqs
 
 
-def slot_sizes(longest, group_tokens, chunk):
-    capacity = TILE
+def needed_modes(longest, rows, heads):
+    own = rows // TILE
+    total = heads
     while True:
-        sizes = {n: min(group_tokens, capacity // n // TILE * TILE) for n in range(1, chunk + 1)}
-
-        def fits(below, above):
-            return any(
-                (n == 0 or below <= sizes[n]) and (n == chunk or above <= sizes[chunk - n])
-                for n in range(chunk + 1)
-            )
-
-        spill = longest - group_tokens - 1
-        if spill <= sizes[chunk] and all(fits(a, longest - a) for a in range(1, longest)):
-            return capacity, sizes
-        capacity += TILE
+        size = {n: min(own, total // n) for n in range(1, heads + 1)}
+        modes, below = [(heads, size[heads], 0)], size[heads] * TILE + 1
+        while below <= rows and longest - below > size[heads] * TILE:
+            found = [
+                (size[n], n) for n in range(1, heads) if size[heads - n] * TILE >= longest - below
+            ]
+            if not found or max(found)[0] * TILE < below:
+                break
+            up, count = max(found)
+            modes.append((count, up, size[heads - count]))
+            below = up * TILE + 1
+        else:
+            if longest - rows - 1 <= size[heads] * TILE:
+                return total, modes + [(0, 0, size[heads])]
+        total += 1
+
+
+def messages(ranks, modes, pairs, base):
+    width = len(ranks) // pairs
+    tables = {True: [], False: []}
+    for upward in tables:
+        for count, up, down in modes:
+            queue, sent = [], []
+            for pair in range(pairs):
+                for head in range(pair * width, (pair + 1) * width):
+                    if (ranks[head] < count) == upward:
+                        queue += [(head, tile) for tile in range(up if upward else down)]
+                room = base if pair < pairs - 1 else len(queue)
+                sent.append(queue[:room])
+                queue = queue[room:]
+            tables[upward].append(sent)
+    return tables
+
+
+def ranked(modes, heads, pairs, base):
+    rng = random.Random(0)
+    width = heads // pairs
+
+    def cost(ranks):
+        worst = late = 0
+        for count, up, down in modes:
+            for upward, size in ((True, up), (False, down)):
+                left = 0
+                for pair in range(pairs):
+                    held = ranks[pair * width:(pair + 1) * width]
+                    left += size * sum((rank < count) == upward for rank in held)
+                    if pair < pairs - 1:
+                        left = max(0, left - base)
+                        late += left
+                worst = max(worst, left)
+        return worst, late
+
+    best = None
+    for _ in range(20):
+        ranks = list(range(heads))
+        rng.shuffle(ranks)
+        now, stall = cost(ranks), 0
+        while stall < 150:
+            i, j = rng.randrange(heads), rng.randrange(heads)
+            ranks[i], ranks[j] = ranks[j], ranks[i]
+            new = cost(ranks)
+            if new <= now:
+                stall = 0 if new < now else stall + 1
+                now = new
+            else:
+                ranks[i], ranks[j] = ranks[j], ranks[i]
+                stall += 1
+        if best is None or now < best[0]:
+            best = (now, list(ranks))
+    return best[1]
+
+
+class Plan:
+    def __init__(self, longest, rows, heads, pairs):
+        self.pairs, self.width = pairs, heads // pairs
+        total, self.modes = needed_modes(longest, rows, heads)
+        base = -(-total // pairs)
+        ranks = ranked(self.modes, heads, pairs, base)
+        self.tables = messages(ranks, self.modes, pairs, base)
+        last = max(len(sent[-1]) for sents in self.tables.values() for sent in sents)
+        self.length = [base] * (pairs - 1) + [last]
+        self.begin = [base * pair for pair in range(pairs)]
+        self.tiles = base * (pairs - 1) + last
+        self.spot, self.until = {}, {}
+        for upward, sents in self.tables.items():
+            self.until[upward] = [0] * pairs
+            for mode, sent in enumerate(sents):
+                for number, tiles in enumerate(sent):
+                    for place, (head, tile) in enumerate(tiles):
+                        self.spot[upward, mode, head, tile] = self.begin[number] + place
+                        pair = head // self.width
+                        self.until[upward][pair] = max(self.until[upward][pair], number)
+            for pair in range(1, pairs):
+                self.until[upward][pair] = max(self.until[upward][pair - 1:pair + 1])
+            self.until[upward][-1] = pairs - 1
+        self.low = [max(up for count, up, _ in self.modes if rank < count) * TILE for rank in ranks]
+        self.high = [max(dn for count, _, dn in self.modes if rank >= count) * TILE for rank in ranks]
+        self.window = rows + max(low + high for low, high in zip(self.low, self.high))
+        self.padded = -(-self.window // LANES) * LANES
+        self.span = max(3 * rows, rows - min(self.low) + self.padded)
 
 
 def dot(left, right, left_dim, right_dim):
@@ -69,12 +161,11 @@
     gain_send, gain_recv,
     halo_send, halo_recv, beside_send, beside_recv,
 ):
-    n, replicas, heads, tok, clips, reach, capacity, slots, window, padded = sizes
+    n, replicas, heads, tok, clips, reach, plan = sizes
     members = n // GROUPS
     group_tokens = members * tok
     chunks = heads // CHUNK
-    low = [slots[index + 1] for index in range(CHUNK)]
-    own_end = [below + group_tokens for below in low]
+    window, padded = plan.window, plan.padded
     feature = members * heads * HEAD_DIM
     ratio = GROUPS
     shared = heads // ratio
@@ -96,8 +187,8 @@
     def columns(owner, head):
         return pl.ds(pl.multiple_of((owner * heads + head) * HEAD_DIM, HEAD_DIM), HEAD_DIM)
 
-    def rows(owner, index):
-        return pl.ds(pl.multiple_of(low[index] + owner * tok, TILE), tok)
+    def rows(owner):
+        return pl.ds(pl.multiple_of(group_tokens + owner * tok, TILE), tok)
 
     def each_side(act):
         @pl.when(side > 0)
@@ -129,11 +220,11 @@
         pl.semaphore_signal(barrier, inc=1, device_id=(other, me), device_id_type=MESH)
     pl.semaphore_wait(barrier, n - 1 + replicas - 1)
 
-    def send_values(head, index):
+    def send_values(head):
         cols = columns(place_in, head)
         for place, ref in ((2, v_ref), (3, do_ref)):
             pltpu.make_async_copy(
-                ref.at[:, cols], recv.at[head, place, rows(place_in, index), :], own_sem.at[head]
+                ref.at[:, cols], recv.at[head, place, rows(place_in), :], own_sem.at[head]
             ).start()
 
         @pl.loop(1, members)
@@ -141,13 +232,13 @@
             other = member(step)
             for place, ref in ((2, v_ref), (3, do_ref)):
                 remote(
-                    ref.at[:, columns(other, head)], recv.at[head, place, rows(place_in, index), :],
+                    ref.at[:, columns(other, head)], recv.at[head, place, rows(place_in), :],
                     in_send.at[head], in_recv.at[head], device(side, other),
                 ).start()
 
     ahead = min(AHEAD, chunks)
     for head in range(ahead * CHUNK):
-        send_values(head, head % CHUNK)
+        send_values(head)
 
     held = jnp.concatenate([pos_ref[axis] for axis in range(3)], axis=0)
     angle = lax.dot_general(
@@ -190,7 +281,7 @@
                 sent[head, other, 0] = rotated(q_ref, gq_ref, scale_q, cols)
                 sent[head, other, 1] = rotated(k_ref, gk_ref, scale_k, cols)
                 remote(
-                    sent.at[head, other], recv.at[head, 0:2, rows(place_in, index), :],
+                    sent.at[head, other], recv.at[head, 0:2, rows(place_in), :],
                     in_send.at[head], in_recv.at[head], device(side, other),
                 ).start()
 
@@ -198,12 +289,12 @@
             for place, (ref, gain, norm) in enumerate(
                 ((q_ref, gq_ref, scale_q), (k_ref, gk_ref, scale_k))
             ):
-                recv[head, place, rows(place_in, index), :] = rotated(ref, gain, norm, cols)
+                recv[head, place, rows(place_in), :] = rotated(ref, gain, norm, cols)
 
         @pl.when(chunk + ahead < chunks)
         def _():
             for index in range(CHUNK):
-                send_values((chunk + ahead) * CHUNK + index, index)
+                send_values((chunk + ahead) * CHUNK + index)
 
     bounds = []
     running = len_ref[0, 0]
@@ -218,36 +309,28 @@
             first = jnp.maximum(first, jnp.where(bound <= middle, bound, 0))
             last = jnp.minimum(last, jnp.where(bound > middle, bound, n * tok))
         below, above = middle - first, last - middle
-        mode = jnp.int32(0)
-        for count in range(1, CHUNK + 1):
-            fits = below <= slots[count]
-            if count < CHUNK:
-                fits = fits & (above <= slots[CHUNK - count])
-            mode = jnp.where(fits, count, mode)
+        mode = jnp.int32(len(plan.modes) - 1)
+        for number in reversed(range(len(plan.modes) - 1)):
+            count, up, down = plan.modes[number]
+            fits = below <= up * TILE
+            if count < heads:
+                fits = fits & (above <= down * TILE)
+            mode = jnp.where(fits, number, mode)
         return first, last, mode
 
     token_start = side * group_tokens
     straddles = straddle(token_start), straddle(token_start + group_tokens)
 
-    def clear(index, begin, end):
-        @pl.loop(0, chunks)
-        def _(chunk):
-            recv[chunk * CHUNK + index, :, begin:end, :] = jnp.zeros(
-                (4, end - begin, HEAD_DIM), jnp.bfloat16
-            )
-
-    for index in range(CHUNK):
-        above = own_end[index] + slots[CHUNK - index]
-        if padded > above:
-            clear(index, above, padded)
-
-        @pl.when(side == 0)
-        def _():
-            clear(index, 0, low[index])
-
-        @pl.when(side == GROUPS - 1)
-        def _():
-            clear(index, own_end[index], above)
+    def clear(begin, end):
+        @pl.loop(0, heads)
+        def _(head):
+            recv[head, :, begin:end, :] = jnp.zeros((4, end - begin, HEAD_DIM), jnp.bfloat16)
+
+    clear(2 * group_tokens, plan.span)
+
+    @pl.when(side == 0)
+    def _():
+        clear(0, group_tokens)
 
     def segment(shape, dim, start, shift):
         inside = lax.broadcasted_iota(jnp.int32, shape, dim) + start
@@ -258,49 +341,45 @@
         valid = (inside < window) & (places >= 0) & (places < n * tok)
         return jnp.where(valid, found, -1)
 
-    def taken(upward):
-        table = []
-        for mode in range(CHUNK + 1):
-            if upward:
-                size = slots[mode] if mode else 0
-                table.append([(index, index * size, size) for index in range(mode)])
-            else:
-                size = slots[CHUNK - mode] if mode < CHUNK else 0
-                table.append([(index, (index - mode) * size, size) for index in range(mode, CHUNK)])
-        return table
-
-    def place_of(upward, halo, index, size):
-        if upward:
-            return (low[index] if halo else own_end[index]) - size
-        return own_end[index] if halo else low[index]
-
-    def modes(which):
+    def masks_of(which):
         held = jnp.full((TILE, HEAD_DIM), straddles[which][2], jnp.int32)
-        return [held == mode for mode in range(CHUNK + 1)]
-
-    def gather(target, source, which, upward, halo, chunk):
-        masks = modes(which)
+        return [held == mode for mode in range(len(plan.modes))]
+
+    def row_of(upward, mode, tile):
+        return (group_tokens if upward else 0) + (tile - (plan.modes[mode][1] if upward else 0)) * TILE
+
+    def select(choices, masks):
+        (value, _), *others = choices
+        for other, modes in others:
+            for mode in modes:
+                value = jnp.where(masks[mode], other, value)
+        return value
+
+    def gather(target, source, which, upward, region, pair):
+        masks = masks_of(which)
 
         @pl.loop(0, 4)
         def _(place):
-            for begin in range(0, capacity, TILE):
-                value = None
-                for mode, table in enumerate(taken(upward)):
-                    for index, start, size in table:
-                        if start <= begin < start + size:
-                            row = place_of(upward, halo, index, size) + begin - start
-                            found = source[chunk * CHUNK + index, place, row:row + TILE, :]
-                            value = found if value is None else jnp.where(masks[mode], found, value)
-                if value is None:
-                    value = jnp.zeros((TILE, HEAD_DIM), jnp.bfloat16)
-                target[chunk, which, place, begin:begin + TILE, :] = value
-
-    def scatter(source, target, which, upward, halo, chunk):
-        masks = modes(which)
+            for spot in range(plan.length[pair]):
+                wanted = {}
+                for mode, sent in enumerate(plan.tables[upward]):
+                    if spot < len(sent[pair]):
+                        head, tile = sent[pair][spot]
+                        wanted.setdefault((head, row_of(upward, mode, tile)), []).append(mode)
+                ordered = sorted(wanted.items(), key=lambda item: -len(item[1]))
+                choices = [
+                    (source[head, place, region + row:region + row + TILE, :], modes)
+                    for (head, row), modes in ordered
+                ]
+                start = (plan.begin[pair] + spot) * TILE
+                target[which, place, start:start + TILE, :] = select(choices, masks)
+
+    def scatter(source, target, which, upward, region, pair, merged):
+        masks = masks_of(which)
         first, last, mode_now = straddles[which]
         lane_rows = lax.broadcasted_iota(jnp.int32, (TILE, HEAD_DIM), 0)
         limits = []
-        for mode in range(CHUNK + 1):
+        for mode in range(len(plan.modes)):
             if upward:
                 limits.append(jnp.where(mode_now == mode, first, n * tok))
             else:
@@ -308,84 +387,107 @@
 
         @pl.loop(0, 4)
         def _(place):
-            for index in range(CHUNK):
-                span = slots[index + 1] if upward else slots[CHUNK - index]
-                base = place_of(upward, halo, index, span)
-                for row in range(base, base + span, TILE):
-                    value = None if halo else target[chunk * CHUNK + index, place, row:row + TILE, :]
-                    tokens = lane_rows + (token_start + row - low[index])
-                    for mode, table in enumerate(taken(upward)):
-                        for owner, start, size in table:
-                            begin = place_of(upward, halo, owner, size)
-                            if owner == index and begin <= row < begin + size:
-                                offset = start + row - begin
-                                found = source[chunk, which, place, offset:offset + TILE, :]
-                                if halo:
-                                    mask = masks[mode]
-                                elif upward:
-                                    mask = tokens >= limits[mode]
-                                else:
-                                    mask = tokens < limits[mode]
-                                value = found if value is None else jnp.where(mask, found, value)
-                    target[chunk * CHUNK + index, place, row:row + TILE, :] = value
-
-    def relay(chunk):
-        for index in range(CHUNK):
-            head = chunk * CHUNK + index
+            for head in range(pair * plan.width, (pair + 1) * plan.width):
+                wanted = {}
+                for mode, (_, up, down) in enumerate(plan.modes):
+                    for tile in range(up if upward else down):
+                        spot = plan.spot.get((upward, mode, head, tile))
+                        if spot is not None:
+                            row = row_of(upward, mode, tile)
+                            wanted.setdefault(row, {}).setdefault(spot, []).append(mode)
+                for row, spots in wanted.items():
+                    ordered = sorted(spots.items(), key=lambda item: -len(item[1]))
+                    choices = [
+                        (source[which, place, spot * TILE:(spot + 1) * TILE, :], modes)
+                        for spot, modes in ordered
+                    ]
+                    here = region + row
+                    if merged:
+                        tokens = lane_rows + (token_start + row)
+                        inside = [tokens >= limit if upward else tokens < limit for limit in limits]
+                        own = target[head, place, here:here + TILE, :]
+                        value = select([(own, [])] + choices, inside)
+                    else:
+                        value = select(choices, masks)
+                    target[head, place, here:here + TILE, :] = value
+
+    def part_of(ref, which, pair):
+        return ref.at[which, :, pl.ds(plan.begin[pair] * TILE, plan.length[pair] * TILE), :]
+
+    def wait_messages(ref, sem, which, upward, pair):
+        begin = plan.until[upward][pair - 1] + 1 if pair else 0
+        for number in range(begin, plan.until[upward][pair] + 1):
+            held = part_of(ref, which, number)
+            pltpu.make_async_copy(held, held, sem.at[which, number]).wait()
+
+    def relay(pair):
+        for head in range(pair * plan.width, (pair + 1) * plan.width):
             arrived = recv.at[head, :, pl.ds(0, (members - 1) * tok), :]
             pltpu.make_async_copy(arrived, arrived, in_recv.at[head]).wait()
             own = recv.at[head, pl.ds(2, 2), pl.ds(0, tok), :]
             pltpu.make_async_copy(own, own, own_sem.at[head]).wait()
 
         def act(which, group):
-            gather(give, recv, which, which == 1, False, chunk)
+            gather(give, recv, which, which == 1, group_tokens, pair)
             remote(
-                give.at[chunk, which], take.at[chunk, 1 - which],
-                halo_send.at[which, chunk], halo_recv.at[1 - which, chunk], device(group, place_in),
+                part_of(give, which, pair), part_of(take, 1 - which, pair),
+                halo_send.at[which, pair], halo_recv.at[1 - which, pair], device(group, place_in),
             ).start()
 
         each_side(act)
 
+    def arrive(pair):
+        def act(which, group):
+            upward = which == 0
+            wait_messages(take, halo_recv, which, upward, pair)
+            scatter(take, recv, which, upward, 0 if upward else 2 * group_tokens, pair, False)
+
+        each_side(act)
+
     def attend(chunk):
-        def arrive(which, group):
-            held = take.at[chunk, which]
-            pltpu.make_async_copy(held, held, halo_recv.at[which, chunk]).wait()
-            scatter(take, recv, which, which == 0, True, chunk)
-
-        each_side(arrive)
-
         @pl.loop(0, CHUNK)
         def _(index):
-            shift = jnp.int32(low[0])
-            for other in range(1, CHUNK):
-                shift = jnp.where(index == other, low[other], shift)
-            attend_head(chunk * CHUNK + index, shift)
-
+            head = chunk * CHUNK + index
+            shift = jnp.int32(plan.low[0])
+            for other in range(1, heads):
+                shift = jnp.where(head == other, plan.low[other], shift)
+            attend_head(head, shift)
+
+    def give_results(pair):
         def act(which, group):
-            gather(give_back, back, which, which == 0, True, chunk)
+            upward = which == 0
+            gather(give_back, back, which, upward, 0 if upward else 2 * group_tokens, pair)
             remote(
-                give_back.at[chunk, which], take_back.at[chunk, 1 - which],
-                beside_send.at[which, chunk], beside_recv.at[1 - which, chunk],
+                part_of(give_back, which, pair), part_of(take_back, 1 - which, pair),
+                beside_send.at[which, pair], beside_recv.at[1 - which, pair],
                 device(group, place_in),
             ).start()
 
         each_side(act)
 
     def attend_head(head, shift):
-        key_acc[...] = jnp.zeros_like(key_acc)
-        value_acc[...] = jnp.zeros_like(value_acc)
-        for start in range(0, window, QUERY_BLOCK):
-            block = min(QUERY_BLOCK, window - start)
+        base = group_tokens - shift
+
+        def at(start, size):
+            return pl.ds(pl.multiple_of(base + start, TILE), size)
+
+        whole = window * padded <= WHOLE_SCORES
+        step_rows = window if whole else QUERY_BLOCK
+        if not whole:
+            key_acc[...] = jnp.zeros_like(key_acc)
+            value_acc[...] = jnp.zeros_like(value_acc)
+        for start in range(0, window, step_rows):
+            block = min(step_rows, window - start)
             first = max(0, start - reach) // LANES * LANES
             last = min(padded, -(-(start + block + reach) // LANES) * LANES)
-            query = recv[head, 0, start:start + block, :]
-            keys = recv[head, 1, first:last, :]
-            value_rows = recv[head, 2, first:last, :]
-            cot = recv[head, 3, start:start + block, :]
+            query = recv[head, 0, at(start, block), :]
+            keys = recv[head, 1, at(first, last - first), :]
+            value_rows = recv[head, 2, at(first, last - first), :]
+            cot = recv[head, 3, at(start, block), :]
             live = segment((block, 1), 0, start, shift) == segment((1, last - first), 1, first, shift)
             scores = jnp.where(live, dot(query, keys, 1, 1), -1e30)
             highest = jnp.max(scores, axis=1, keepdims=True)
-            expon = jnp.exp((scores - highest) * scale)
+            expon = jnp.exp2((scores - highest) * (scale * LOG2_E))
             probs = expon * (1.0 / jnp.sum(expon, axis=1, keepdims=True))
             half = probs.astype(jnp.bfloat16)
             context = dot(half, value_rows, 1, 0).astype(jnp.bfloat16)
@@ -393,21 +495,30 @@
                 cot.astype(jnp.float32) * context.astype(jnp.float32), axis=1, keepdims=True
             )
             dprob = dot(cot, value_rows, 1, 1)
-            dscore = (probs * (dprob - delta) * scale).astype(jnp.bfloat16)
-            back[head, 2, start:start + block, :] = context
-            back[head, 0, start:start + block, :] = dot(dscore, keys, 1, 0).astype(jnp.bfloat16)
-            key_acc[first:last, :] += dot(dscore, query, 0, 0)
-            value_acc[first:last, :] += dot(half, cot, 0, 0)
-        back[head, 1] = key_acc[0:window, :].astype(jnp.bfloat16)
-        back[head, 3] = value_acc[0:window, :].astype(jnp.bfloat16)
+            dscore = (probs * (dprob - delta)).astype(jnp.bfloat16)
+            back[head, 2, at(start, block), :] = context
+            back[head, 0, at(start, block), :] = (dot(dscore, keys, 1, 0) * scale).astype(jnp.bfloat16)
+            key_part = (dot(query, dscore, 0, 0) * scale).T
+            value_part = dot(cot, half, 0, 0).T
+            if whole:
+                back[head, 1, at(0, window), :] = key_part[0:window].astype(jnp.bfloat16)
+                back[head, 3, at(0, window), :] = value_part[0:window].astype(jnp.bfloat16)
+            else:
+                key_acc[first:last, :] += key_part
+                value_acc[first:last, :] += value_part
+        if not whole:
+            back[head, 1, at(0, window), :] = key_acc[0:window, :].astype(jnp.bfloat16)
+            back[head, 3, at(0, window), :] = value_acc[0:window, :].astype(jnp.bfloat16)
+
+    def merge(pair):
+        def act(which, group):
+            upward = which == 1
+            wait_messages(take_back, beside_recv, which, upward, pair)
+            scatter(take_back, back, which, upward, group_tokens, pair, True)
+
+        each_side(act)
 
     def distribute(chunk):
-        def merge(which, group):
-            held = take_back.at[chunk, which]
-            pltpu.make_async_copy(held, held, beside_recv.at[which, chunk]).wait()
-            scatter(take_back, back, which, which == 1, False, chunk)
-
-        each_side(merge)
         outward(chunk, 0, (dq_ref, dk_ref), out_send, out_recv)
 
         @pl.when(chunk < chunks - DEFERRED)
@@ -424,12 +535,12 @@
                 other = member(step)
                 for place, target in enumerate(targets):
                     remote(
-                        back.at[head, first + place, rows(other, index), :], target.at[:, cols],
+                        back.at[head, first + place, rows(other), :], target.at[:, cols],
                         send.at[head], receive.at[head], device(side, other),
                     ).start()
 
             for place, target in enumerate(targets):
-                target[:, cols] = back[head, first + place, rows(place_in, index), :]
+                target[:, cols] = back[head, first + place, rows(place_in), :]
 
     def arrived_pair(head, sem):
         held = recv.at[head, 0:2, pl.ds(0, (members - 1) * tok), :]
@@ -465,19 +576,27 @@
 
     @pl.loop(0, chunks + ATTEND_LAG + DISTRIBUTE_LAG + NORM_LAG)
     def _(step):
-        @pl.when(step < chunks)
+        def each_pair(now, act):
+            for pair in range(chunks):
+                @pl.when(now == pair)
+                def _():
+                    act(pair)
+
+        each_pair(step, relay)
+        attended = step - ATTEND_LAG
+        each_pair(attended, arrive)
+
+        @pl.when((attended >= 0) & (attended < chunks))
         def _():
-            relay(step)
-
-        @pl.when((step >= ATTEND_LAG) & (step < chunks + ATTEND_LAG))
+            attend(attended)
+
+        each_pair(attended, give_results)
+        merged = attended - DISTRIBUTE_LAG
+        each_pair(merged, merge)
+
+        @pl.when((merged >= 0) & (merged < chunks))
         def _():
-            attend(step - ATTEND_LAG)
-
-        @pl.when(
-            (step >= ATTEND_LAG + DISTRIBUTE_LAG) & (step < chunks + ATTEND_LAG + DISTRIBUTE_LAG)
-        )
-        def _():
-            distribute(step - ATTEND_LAG - DISTRIBUTE_LAG)
+            distribute(merged)
 
         @pl.when(step >= ATTEND_LAG + DISTRIBUTE_LAG + NORM_LAG)
         def _():
@@ -550,12 +669,11 @@
         arrived_pair(head, late_send)
         arrived_pair(head, late_recv)
 
-    @pl.loop(0, chunks)
-    def _(chunk):
+    for pair in range(chunks):
         def drain(which, group):
-            held = give.at[chunk, which]
-            pltpu.make_async_copy(held, held, halo_send.at[which, chunk]).wait()
-            pltpu.make_async_copy(held, held, beside_send.at[which, chunk]).wait()
+            held = part_of(give, which, pair)
+            pltpu.make_async_copy(held, held, halo_send.at[which, pair]).wait()
+            pltpu.make_async_copy(held, held, beside_send.at[which, pair]).wait()
 
         each_side(drain)
 
@@ -588,10 +706,8 @@
     reach = tokens // 3 - 1
     group_tokens = tokens // GROUPS
     chunks = heads // CHUNK
-    capacity, slots = slot_sizes(reach + 1, group_tokens, CHUNK)
-    window = group_tokens + max(slots[i + 1] + slots[CHUNK - i] for i in range(CHUNK))
-    padded = -(-window // LANES) * LANES
-    sizes = (n, replicas, heads, tok, lengths.shape[1], reach, capacity, slots, window, padded)
+    plan = Plan(reach + 1, group_tokens, heads, chunks)
+    sizes = (n, replicas, heads, tok, lengths.shape[1], reach, plan)
     vmem = pl.BlockSpec(memory_space=pltpu.VMEM)
     hbm = pl.BlockSpec(memory_space=pl.ANY)
     gain_rows = (2 * shared, LANES)
@@ -613,15 +729,15 @@
             pltpu.VMEM((tok, HEAD_DIM), full),
             pltpu.VMEM((tok, LANES), full),
             pltpu.VMEM((tok, LANES), full),
-            pltpu.VMEM((chunks, 2, 4, capacity, HEAD_DIM), half),
-            pltpu.VMEM((chunks, 2, 4, capacity, HEAD_DIM), half),
-            pltpu.VMEM((chunks, 2, 4, capacity, HEAD_DIM), half),
-            pltpu.VMEM((chunks, 2, 4, capacity, HEAD_DIM), half),
+            pltpu.VMEM((2, 4, plan.tiles * TILE, HEAD_DIM), half),
+            pltpu.VMEM((2, 4, plan.tiles * TILE, HEAD_DIM), half),
+            pltpu.VMEM((2, 4, plan.tiles * TILE, HEAD_DIM), half),
+            pltpu.VMEM((2, 4, plan.tiles * TILE, HEAD_DIM), half),
             pltpu.VMEM((heads, n // GROUPS, 2, tok, HEAD_DIM), half),
-            pltpu.VMEM((heads, 4, padded, HEAD_DIM), half),
-            pltpu.VMEM((heads, 4, window, HEAD_DIM), half),
-            pltpu.VMEM((padded, HEAD_DIM), full),
-            pltpu.VMEM((padded, HEAD_DIM), full),
+            pltpu.VMEM((heads, 4, plan.span, HEAD_DIM), half),
+            pltpu.VMEM((heads, 4, plan.span, HEAD_DIM), half),
+            pltpu.VMEM((plan.padded, HEAD_DIM), full),
+            pltpu.VMEM((plan.padded, HEAD_DIM), full),
             pltpu.VMEM((tok, LANES), full),
             pltpu.VMEM((tok, LANES), full),
             pltpu.VMEM((n,) + gain_rows, full),

time: 121 us -> 115 us (0.950)
  Pallas kernels: 120 us -> 114 us
    pallas_call x1, Pallas kernels: 118 us -> 111 us  [on_device(): pl.pallas_call(functools.partial(kernel, sizes), out_shape=(*[pltpu.VMEM(...]
where the time goes in v4:
time: 115 us
  Pallas kernels  114 us (99%)
    pallas_call x1, Pallas kernels, on_device(): pl.pallas_call(functools.partial(kernel, sizes), out_shape=(*[pltpu.VMEM(...  111 us
    pallas_call x1, Pallas kernels, on_device(): pl.pallas_call(finish, out_shape=(jax.ShapeDtypeStruct((tok, feature), ha...  2.65 us

profile of v4, /device:TPU:0, one launch (start us, length us, event | category | flops | bytes accessed | tf_op | source)
XLA Modules:
  0.0 114.7 jit_solution(5765560785468925541)
XLA Ops:
  0.6 111.4 %shard_map.136 = (bf16[128,4096]{1,0:T(8,128)(2,1)S(1)}, bf16[128,4096]{1,0:T(8,128)(2,1)S(1)}, bf16[128,4096]{1,0:T(8,128)(2,1)S(1)}, bf16[128,4096]{1,0:T(8,128)(2,1)S(1)}, f32[8,8,128]{2,1,0:T(8,128)S(1)}) custom-call(s32[1,6]{1,0:T(1,128)} %len_ref.1, bf16[128,4096]{1,0:T(8,128)(2,1)} %bitcast.13, bf16[128,4096]{1,0:T(8,128)(2,1)} %bitcast.14, ...), custom_call_target="tpu_custom_call" | custom-call | tf_op jit(solution)/shard_map/pallas_call | solution.py:715
  112.0 2.7 %shard_map.137 = (bf16[128,4096]{1,0:T(8,128)(2,1)}, bf16[128,4096]{1,0:T(8,128)(2,1)}, bf16[128,4096]{1,0:T(8,128)(2,1)}, bf16[128,4096]{1,0:T(8,128)(2,1)}, f32[1,4096]{1,0:T(1,128)}, /*index=5*/f32[1,4096]{1,0:T(1,128)}) custom-call(f32[8,8,128]{2,1,0:T(8,128)S(1)} %get-tuple-element.17.gains_ref, bf16[128,4096]{1,0:T(8,128)(2,1)S(1)} %get-tuple-element.18.refs_0_, ...), custom_call_target="tpu_custom_call" | custom-call | tf_op jit(solution)/shard_map/pallas_call | solution.py:770

commit v5 on v4

--- a/solution.py
+++ b/solution.py
@@ -22,6 +22,7 @@
 NORM_LAG = 1
 DEFERRED = 2
 AHEAD = 1
+SENT_AHEAD = 8
 EPSILON = 1e-06
 MESH = pl.DeviceIdType.MESH
 
@@ -213,12 +214,17 @@
         load.start()
 
     barrier = pltpu.get_barrier_semaphore()
-    for step in range(1, n):
-        pl.semaphore_signal(barrier, inc=1, device_id=(my_dp, peer(step)), device_id_type=MESH)
+
+    def greet(target):
+        pl.semaphore_signal(barrier, inc=1, device_id=target, device_id_type=MESH)
+
+    for step in range(1, members):
+        greet(device(side, member(step)))
     for step in range(1, replicas):
-        other = lax.rem(my_dp + step, replicas)
-        pl.semaphore_signal(barrier, inc=1, device_id=(other, me), device_id_type=MESH)
-    pl.semaphore_wait(barrier, n - 1 + replicas - 1)
+        greet((lax.rem(my_dp + step, replicas), me))
+    each_side(lambda which, group: greet(device(group, place_in)))
+    sides_here = jnp.minimum(side, 1) + jnp.minimum(GROUPS - 1 - side, 1)
+    pl.semaphore_wait(barrier, members - 1 + replicas - 1 + sides_here)
 
     def send_values(head):
         cols = columns(place_in, head)
@@ -233,7 +239,7 @@
             for place, ref in ((2, v_ref), (3, do_ref)):
                 remote(
                     ref.at[:, columns(other, head)], recv.at[head, place, rows(place_in), :],
-                    in_send.at[head], in_recv.at[head], device(side, other),
+                    in_send.at[0], in_recv.at[head], device(side, other),
                 ).start()
 
     ahead = min(AHEAD, chunks)
@@ -269,8 +275,7 @@
         turned = x * cos_ref[...] + pltpu.roll(x, HEAD_DIM // 2, 1) * sin_ref[...]
         return turned.astype(jnp.bfloat16)
 
-    @pl.loop(0, chunks)
-    def _(chunk):
+    def send_pair(chunk):
         for index in range(CHUNK):
             head = chunk * CHUNK + index
 
@@ -282,7 +287,7 @@
                 sent[head, other, 1] = rotated(k_ref, gk_ref, scale_k, cols)
                 remote(
                     sent.at[head, other], recv.at[head, 0:2, rows(place_in), :],
-                    in_send.at[head], in_recv.at[head], device(side, other),
+                    in_send.at[0], in_recv.at[head], device(side, other),
                 ).start()
 
             cols = columns(place_in, head)
@@ -295,6 +300,10 @@
         def _():
             for index in range(CHUNK):
                 send_values((chunk + ahead) * CHUNK + index)
+
+    @pl.loop(0, min(SENT_AHEAD, chunks))
+    def _(chunk):
+        send_pair(chunk)
 
     bounds = []
     running = len_ref[0, 0]
@@ -431,7 +440,7 @@
             gather(give, recv, which, which == 1, group_tokens, pair)
             remote(
                 part_of(give, which, pair), part_of(take, 1 - which, pair),
-                halo_send.at[which, pair], halo_recv.at[1 - which, pair], device(group, place_in),
+                halo_send.at[which], halo_recv.at[1 - which, pair], device(group, place_in),
             ).start()
 
         each_side(act)
@@ -459,7 +468,7 @@
             gather(give_back, back, which, upward, 0 if upward else 2 * group_tokens, pair)
             remote(
                 part_of(give_back, which, pair), part_of(take_back, 1 - which, pair),
-                beside_send.at[which, pair], beside_recv.at[1 - which, pair],
+                beside_send.at[which], beside_recv.at[1 - which, pair],
                 device(group, place_in),
             ).start()
 
@@ -519,13 +528,13 @@
         each_side(act)
 
     def distribute(chunk):
-        outward(chunk, 0, (dq_ref, dk_ref), out_send, out_recv)
+        outward(chunk, 0, (dq_ref, dk_ref), out_send, out_recv, True)
 
         @pl.when(chunk < chunks - DEFERRED)
         def _():
-            outward(chunk, 2, (att_ref, dv_ref), late_send, late_recv)
-
-    def outward(chunk, first, targets, send, receive):
+            outward(chunk, 2, (att_ref, dv_ref), late_send, late_recv, False)
+
+    def outward(chunk, first, targets, send, receive, each):
         for index in range(CHUNK):
             head = chunk * CHUNK + index
             cols = columns(place_in, head)
@@ -536,7 +545,7 @@
                 for place, target in enumerate(targets):
                     remote(
                         back.at[head, first + place, rows(other), :], target.at[:, cols],
-                        send.at[head], receive.at[head], device(side, other),
+                        send.at[0], receive.at[head if each else 0], device(side, other),
                     ).start()
 
             for place, target in enumerate(targets):
@@ -583,6 +592,11 @@
                     act(pair)
 
         each_pair(step, relay)
+
+        @pl.when(step + SENT_AHEAD < chunks)
+        def _():
+            send_pair(step + SENT_AHEAD)
+
         attended = step - ATTEND_LAG
         each_pair(attended, arrive)
 
@@ -616,7 +630,7 @@
 
     @pl.loop(chunks - min(DEFERRED, chunks), chunks)
     def _(chunk):
-        outward(chunk, 2, (att_ref, dv_ref), late_send, late_recv)
+        outward(chunk, 2, (att_ref, dv_ref), late_send, late_recv, False)
 
     means = [
         jnp.broadcast_to(jnp.sum(inner[...], axis=1, keepdims=True) / feature, (tok, LANES))
@@ -661,21 +675,18 @@
     wait_all(seq_part, n - 1, gain_send.at[1])
     wait_all(dp_part, replicas - 1, gain_send.at[2])
 
-    @pl.loop(0, heads)
-    def _(head):
-        moved = recv.at[head, :, pl.ds(0, (members - 1) * tok), :]
-        pltpu.make_async_copy(moved, moved, in_send.at[head]).wait()
-        arrived_pair(head, out_send)
-        arrived_pair(head, late_send)
-        arrived_pair(head, late_recv)
-
-    for pair in range(chunks):
-        def drain(which, group):
-            held = part_of(give, which, pair)
-            pltpu.make_async_copy(held, held, halo_send.at[which, pair]).wait()
-            pltpu.make_async_copy(held, held, beside_send.at[which, pair]).wait()
-
-        each_side(drain)
+    moved = recv.at[:, :, pl.ds(0, (members - 1) * tok), :]
+    pltpu.make_async_copy(moved, moved, in_send.at[0]).wait()
+    halves = recv.at[:, 0:2, pl.ds(0, (members - 1) * tok), :]
+    for sem in (out_send, late_send, late_recv):
+        pltpu.make_async_copy(halves, halves, sem.at[0]).wait()
+
+    def drain(which, group):
+        held = give.at[which]
+        pltpu.make_async_copy(held, held, halo_send.at[which]).wait()
+        pltpu.make_async_copy(held, held, beside_send.at[which]).wait()
+
+    each_side(drain)
 
 
 def finish(gains_ref, *refs):
@@ -746,18 +757,18 @@
             pltpu.VMEM((replicas, n // replicas) + gain_rows, full),
             pltpu.VMEM((n // replicas,) + gain_rows, full),
             pltpu.SemaphoreType.DMA((2,)),
+            pltpu.SemaphoreType.DMA((1,)),
             pltpu.SemaphoreType.DMA((heads,)),
             pltpu.SemaphoreType.DMA((heads,)),
+            pltpu.SemaphoreType.DMA((1,)),
             pltpu.SemaphoreType.DMA((heads,)),
-            pltpu.SemaphoreType.DMA((heads,)),
-            pltpu.SemaphoreType.DMA((heads,)),
-            pltpu.SemaphoreType.DMA((heads,)),
-            pltpu.SemaphoreType.DMA((heads,)),
+            pltpu.SemaphoreType.DMA((1,)),
+            pltpu.SemaphoreType.DMA((1,)),
             pltpu.SemaphoreType.DMA((3,)),
             pltpu.SemaphoreType.DMA((3,)),
+            pltpu.SemaphoreType.DMA((2,)),
             pltpu.SemaphoreType.DMA((2, chunks)),
-            pltpu.SemaphoreType.DMA((2, chunks)),
-            pltpu.SemaphoreType.DMA((2, chunks)),
+            pltpu.SemaphoreType.DMA((2,)),
             pltpu.SemaphoreType.DMA((2, chunks)),
         ],
         compiler_params=pltpu.CompilerParams(

time: 115 us -> 113 us (0.983)
  Pallas kernels: 114 us -> 112 us
    pallas_call x1, Pallas kernels: 111 us -> 110 us  [on_device(): pl.pallas_call(functools.partial(kernel, sizes), out_shape=(*[pltpu.VMEM(...]
where the time goes in v5:
time: 113 us
  Pallas kernels  112 us (99%)
    pallas_call x1, Pallas kernels, on_device(): pl.pallas_call(functools.partial(kernel, sizes), out_shape=(*[pltpu.VMEM(...  110 us
    pallas_call x1, Pallas kernels, on_device(): pl.pallas_call(finish, out_shape=(jax.ShapeDtypeStruct((tok, feature), ha...  2.65 us

profile of v5, /device:TPU:0, one launch (start us, length us, event | category | flops | bytes accessed | tf_op | source)
XLA Modules:
  0.0 112.9 jit_solution(9123752117097670659)
XLA Ops:
  0.6 109.6 %shard_map.136 = (bf16[128,4096]{1,0:T(8,128)(2,1)S(1)}, bf16[128,4096]{1,0:T(8,128)(2,1)S(1)}, bf16[128,4096]{1,0:T(8,128)(2,1)S(1)}, bf16[128,4096]{1,0:T(8,128)(2,1)S(1)}, f32[8,8,128]{2,1,0:T(8,128)S(1)}) custom-call(s32[1,6]{1,0:T(1,128)} %len_ref.1, bf16[128,4096]{1,0:T(8,128)(2,1)} %bitcast.13, bf16[128,4096]{1,0:T(8,128)(2,1)} %bitcast.14, ...), custom_call_target="tpu_custom_call" | custom-call | tf_op jit(solution)/shard_map/pallas_call | solution.py:726
  110.3 2.7 %shard_map.137 = (bf16[128,4096]{1,0:T(8,128)(2,1)}, bf16[128,4096]{1,0:T(8,128)(2,1)}, bf16[128,4096]{1,0:T(8,128)(2,1)}, bf16[128,4096]{1,0:T(8,128)(2,1)}, f32[1,4096]{1,0:T(1,128)}, /*index=5*/f32[1,4096]{1,0:T(1,128)}) custom-call(f32[8,8,128]{2,1,0:T(8,128)S(1)} %get-tuple-element.17.gains_ref, bf16[128,4096]{1,0:T(8,128)(2,1)S(1)} %get-tuple-element.18.refs_0_, ...), custom_call_target="tpu_custom_call" | custom-call | tf_op jit(solution)/shard_map/pallas_call | solution.py:781

commit v6 on v5

--- a/solution.py
+++ b/solution.py
@@ -628,10 +628,6 @@
         ).start()
     dp_part[my_dp] = part[portion(my_dp)]
 
-    @pl.loop(chunks - min(DEFERRED, chunks), chunks)
-    def _(chunk):
-        outward(chunk, 2, (att_ref, dv_ref), late_send, late_recv, False)
-
     means = [
         jnp.broadcast_to(jnp.sum(inner[...], axis=1, keepdims=True) / feature, (tok, LANES))
         for inner in (inner_q, inner_k)
@@ -659,6 +655,10 @@
         remote(
             dp_sum, seq_part.at[me], gain_send.at[1], gain_recv.at[1], (my_dp, other)
         ).start()
+
+    @pl.loop(chunks - min(DEFERRED, chunks), chunks)
+    def _(chunk):
+        outward(chunk, 2, (att_ref, dv_ref), late_send, late_recv, False)
 
     seq_part[me] = dp_sum[...]
     wait_all(seq_part, n - 1, gain_recv.at[1])

time: 113 us -> 113 us (level)
  no operation moved by 1% of the time
where the time goes in v6:
time: 113 us
  Pallas kernels  112 us (99%)
    pallas_call x1, Pallas kernels, on_device(): pl.pallas_call(functools.partial(kernel, sizes), out_shape=(*[pltpu.VMEM(...  110 us
    pallas_call x1, Pallas kernels, on_device(): pl.pallas_call(finish, out_shape=(jax.ShapeDtypeStruct((tok, feature), ha...  2.65 us

profile of v6, /device:TPU:0, one launch (start us, length us, event | category | flops | bytes accessed | tf_op | source)
XLA Modules:
  0.0 112.9 jit_solution(12851897265591830344)
XLA Ops:
  0.6 109.6 %shard_map.136 = (bf16[128,4096]{1,0:T(8,128)(2,1)S(1)}, bf16[128,4096]{1,0:T(8,128)(2,1)S(1)}, bf16[128,4096]{1,0:T(8,128)(2,1)S(1)}, bf16[128,4096]{1,0:T(8,128)(2,1)S(1)}, f32[8,8,128]{2,1,0:T(8,128)S(1)}) custom-call(s32[1,6]{1,0:T(1,128)} %len_ref.1, bf16[128,4096]{1,0:T(8,128)(2,1)} %bitcast.13, bf16[128,4096]{1,0:T(8,128)(2,1)} %bitcast.14, ...), custom_call_target="tpu_custom_call" | custom-call | tf_op jit(solution)/shard_map/pallas_call | solution.py:726
  110.2 2.7 %shard_map.137 = (bf16[128,4096]{1,0:T(8,128)(2,1)}, bf16[128,4096]{1,0:T(8,128)(2,1)}, bf16[128,4096]{1,0:T(8,128)(2,1)}, bf16[128,4096]{1,0:T(8,128)(2,1)}, f32[1,4096]{1,0:T(1,128)}, /*index=5*/f32[1,4096]{1,0:T(1,128)}) custom-call(f32[8,8,128]{2,1,0:T(8,128)S(1)} %get-tuple-element.17.gains_ref, bf16[128,4096]{1,0:T(8,128)(2,1)S(1)} %get-tuple-element.18.refs_0_, ...), custom_call_target="tpu_custom_call" | custom-call | tf_op jit(solution)/shard_map/pallas_call | solution.py:781
